TPU v7x, 1024 devices: a whole 4x8x16 slice. The times are simulated.
1024 devices in a mesh: tok: 64 (over x, y, core), head: 16 (over z).
Axes of the slice: x: 4, y: 8, z: 16, core: 2. Of those that a mesh axis runs over, the one named last changes fastest.
Arguments:
- query_latent: bfloat16 [8192, 128, 512], P('tok', 'head'), may hold values from -100 to 100
- query_rotary: bfloat16 [8192, 8192], P('tok', 'head'), may hold values from -6 to 6
- latents: bfloat16 [8192, 512], P('tok'), may hold values from -8 to 8
- key_rotary: bfloat16 [8192, 64], P('tok'), may hold values from -6 to 6
- out_grad: bfloat16 [8192, 128, 512], P('tok', 'head'), may hold values from -6 to 6
- doc_lengths: int32 [33], replicated, may hold values from 1 to 384, 8192 in all
Outputs:
- grad_query_latent: bfloat16 [8192, 128, 512], P('tok', 'head')
- grad_query_rotary: bfloat16 [8192, 8192], P('tok', 'head')
- grad_latents: bfloat16 [8192, 512], P(('tok', 'head'))
- grad_key_rotary: bfloat16 [8192, 64], P(('tok', 'head'))
Inputs may be any that keep to these rules, and one draw needn't show every extreme that they name: `doc_lengths`: the lengths sum to 8192, and some document has exactly 384 tokens.
All inputs are finite; a program needn't handle non-finite values.
Results may differ from a plain program's by a relative error of at most 0.013.
Values may be sent and summed in bfloat16 or wider, within the bound.
No kernel may reach another device: no remote copies, remote signals or barrier semaphores. Data moves between devices by JAX's collectives and lax.ppermute only.
A program may use at most 32 MiB of HBM per device.

v0:
```python
import jax
import jax.numpy as jnp
from jax import lax
from jax.sharding import PartitionSpec as P

SPAN = 3


SCALE = 0.07216878364870322
NEGATIVE = -1e30


def shifted(block, axis, distance):
    devices = range(lax.axis_size(axis))
    route = [(i - distance, i) for i in devices if i - distance in devices]
    return lax.ppermute(block, axis, route)


def body(query_latent, query_rotary, latents, key_rotary, out_grad, doc_lengths):
    tok_rows = latents.shape[0]
    head_count = query_latent.shape[1]
    rotary_width = key_rotary.shape[1]
    shard = lax.axis_index("tok")
    offsets = jnp.arange(tok_rows, dtype=jnp.int32)
    query_pos = shard * tok_rows + offsets
    doc_starts = jnp.cumsum(doc_lengths) - doc_lengths
    query_start = jnp.max(
        jnp.where(doc_starts[None, :] <= query_pos[:, None], doc_starts[None, :], 0), axis=1
    )
    latent_tiles = [latents]
    rotary_tiles = [key_rotary]
    place_tiles = [query_pos]
    for distance in range(1, SPAN + 1):
        fetched = shifted((latents, key_rotary), "tok", distance)
        latent_tiles.append(fetched[0])
        rotary_tiles.append(fetched[1])
        place_tiles.append(query_pos - distance * tok_rows)
    key_latent = jnp.concatenate(latent_tiles, axis=0)
    key_rot = jnp.concatenate(rotary_tiles, axis=0)
    key_place = jnp.concatenate(place_tiles, axis=0)
    rotary_query = query_rotary.reshape(tok_rows, head_count, rotary_width)
    visible = (key_place[None, :] >= query_start[:, None]) & (
        key_place[None, :] <= query_pos[:, None]
    )
    scores = SCALE * (
        jnp.einsum("qhd,kd->hqk", query_latent, key_latent, preferred_element_type=jnp.float32)
        + jnp.einsum("qhr,kr->hqk", rotary_query, key_rot, preferred_element_type=jnp.float32)
    )
    masked = jnp.where(visible[None], scores, NEGATIVE)
    row_max = jnp.max(masked, axis=2, keepdims=True)
    exp_terms = jnp.where(visible[None], jnp.exp(masked - row_max), 0.0)
    attn_probs = exp_terms / jnp.sum(exp_terms, axis=2, keepdims=True)
    probs_low = attn_probs.astype(jnp.bfloat16)
    attn_out = jnp.einsum("hqk,kd->qhd", probs_low, key_latent, preferred_element_type=jnp.float32)
    row_delta = jnp.sum(out_grad.astype(jnp.float32) * attn_out, axis=2)
    prob_grad = jnp.einsum("qhd,kd->hqk", out_grad, key_latent, preferred_element_type=jnp.float32)
    score_grad = (attn_probs * (prob_grad - jnp.transpose(row_delta)[:, :, None])).astype(
        jnp.bfloat16
    )
    grad_query_latent = (
        SCALE
        * jnp.einsum("hqk,kd->qhd", score_grad, key_latent, preferred_element_type=jnp.float32)
    ).astype(jnp.bfloat16)
    grad_query_rotary = (
        (SCALE * jnp.einsum("hqk,kr->qhr", score_grad, key_rot, preferred_element_type=jnp.float32))
        .reshape(tok_rows, head_count * rotary_width)
        .astype(jnp.bfloat16)
    )
    latent_grad = SCALE * jnp.einsum(
        "hqk,qhd->kd", score_grad, query_latent, preferred_element_type=jnp.float32
    ) + jnp.einsum("hqk,qhd->kd", probs_low, out_grad, preferred_element_type=jnp.float32)
    rotary_grad = SCALE * jnp.einsum(
        "hqk,qhr->kr", score_grad, rotary_query, preferred_element_type=jnp.float32
    )
    total_latent = latent_grad[:tok_rows]
    total_rotary = rotary_grad[:tok_rows]
    for distance in range(1, SPAN + 1):
        piece_latent = latent_grad[distance * tok_rows : (distance + 1) * tok_rows]
        piece_rotary = rotary_grad[distance * tok_rows : (distance + 1) * tok_rows]
        returned = (
            shifted(piece_latent.astype(jnp.bfloat16), "tok", -distance).astype(piece_latent.dtype),
            shifted(piece_rotary.astype(jnp.bfloat16), "tok", -distance).astype(piece_rotary.dtype),
        )
        total_latent = total_latent + returned[0]
        total_rotary = total_rotary + returned[1]
    summed = (
        lax.psum_scatter(total_latent, "head", scatter_dimension=0, tiled=True),
        lax.psum_scatter(total_rotary, "head", scatter_dimension=0, tiled=True),
    )
    summed_latent = summed[0]
    summed_rotary = summed[1]
    return (
        grad_query_latent,
        grad_query_rotary,
        summed_latent.astype(jnp.bfloat16),
        summed_rotary.astype(jnp.bfloat16),
    )


def solution(mesh):
    in_specs = (
        P("tok", "head", None),
        P("tok", "head"),
        P("tok", None),
        P("tok", None),
        P("tok", "head", None),
        P(),
    )
    out_specs = (
        P("tok", "head", None),
        P("tok", "head"),
        P(("tok", "head"), None),
        P(("tok", "head"), None),
    )
    return jax.shard_map(body, mesh=mesh, in_specs=in_specs, out_specs=out_specs, check_vma=False)
```

profile of v0, /device:TPU:2, one launch (start us, length us, event | category | flops | bytes accessed | tf_op | source)
XLA Modules:
  0.0 164.6 jit_solution(14675972584315759038)
XLA Ops:
  7.2 2.1 %collective-permute-start.3 = (bf16[128,64]{0,1:T(8,128)(2,1)}, bf16[128,64]{0,1:T(8,128)(2,1)S(1)}, u32[]{:S(2)}, u32[]{:S(2)}) collective-permute-start(bf16[128,64]{0,1:T(8,128)(2,1)} %param.9), channel_id=1, source_target_pairs={{0,16},{16,32},{32,48},{48,64},{64,80},{80,96},{96,112},{112,128},... | collective-permute-start | bytes 49160 | tf_op jit(solution)/shard_map/ppermute | solution.py:16
  9.3 3.5 %collective-permute-start.4 = (bf16[128,64]{0,1:T(8,128)(2,1)}, bf16[128,64]{0,1:T(8,128)(2,1)S(1)}, u32[]{:S(2)}, u32[]{:S(2)}) collective-permute-start(bf16[128,64]{0,1:T(8,128)(2,1)} %param.9), channel_id=1, source_target_pairs={{0,32},{16,48},{32,64},{48,80},{64,96},{80,112},{96,128},{112,144}... | collective-permute-start | bytes 49160 | tf_op jit(solution)/shard_map/ppermute | solution.py:16
  12.8 4.5 %collective-permute-start.5 = (bf16[128,64]{0,1:T(8,128)(2,1)}, bf16[128,64]{0,1:T(8,128)(2,1)S(1)}, u32[]{:S(2)}, u32[]{:S(2)}) collective-permute-start(bf16[128,64]{0,1:T(8,128)(2,1)} %param.9), channel_id=1, source_target_pairs={{0,48},{16,64},{32,80},{48,96},{64,112},{80,128},{96,144},{112,160... | collective-permute-start | bytes 49160 | tf_op jit(solution)/shard_map/ppermute | solution.py:16
  17.3 2.0 %collective-permute-start = (bf16[128,512]{1,0:T(8,128)(2,1)}, bf16[128,512]{1,0:T(8,128)(2,1)}, u32[]{:S(2)}, u32[]{:S(2)}) collective-permute-start(bf16[128,512]{1,0:T(8,128)(2,1)} %param.8), channel_id=1, source_target_pairs={{0,16},{16,32},{32,48},{48,64},{64,80},{80,96},{96,112},{112,128},... | collective-permute-start | bytes 393224 | tf_op jit(solution)/shard_map/ppermute | solution.py:16
  19.3 4.7 %collective-permute-start.1 = (bf16[128,512]{1,0:T(8,128)(2,1)}, bf16[128,512]{1,0:T(8,128)(2,1)}, u32[]{:S(2)}, u32[]{:S(2)}) collective-permute-start(bf16[128,512]{1,0:T(8,128)(2,1)} %param.8), channel_id=1, source_target_pairs={{0,32},{16,48},{32,64},{48,80},{64,96},{80,112},{96,128},{112,144}... | collective-permute-start | bytes 393224 | tf_op jit(solution)/shard_map/ppermute | solution.py:16
  24.1 0.8 copy.59
  25.0 0.7 sub.34
  25.9 1.0 copy.61
  26.9 2.7 %copy.63 = bf16[128,8,512]{0,2,1:T(8,128)(2,1)} copy(bf16[128,8,512]{2,1,0:T(8,128)(2,1)} %param.10) | data formatting | bytes 2097152 | tf_op args[4]
  29.6 1.3 dynamic-slice
  31.5 2.6 %collective-permute-start.2 = (bf16[128,512]{1,0:T(8,128)(2,1)}, bf16[128,512]{1,0:T(8,128)(2,1)}, u32[]{:S(2)}, u32[]{:S(2)}) collective-permute-start(bf16[128,512]{1,0:T(8,128)(2,1)} %param.8), channel_id=1, source_target_pairs={{0,48},{16,64},{32,80},{48,96},{64,112},{80,128},{96,144},{112,160... | collective-permute-start | bytes 393224 | tf_op jit(solution)/shard_map/ppermute | solution.py:16
  34.6 8.7 %collective-permute-done.2 = bf16[128,512]{1,0:T(8,128)(2,1)} collective-permute-done((bf16[128,512]{1,0:T(8,128)(2,1)}, bf16[128,512]{1,0:T(8,128)(2,1)}, u32[]{:S(2)}, u32[]{:S(2)}) %collective-permute-start.2) | collective-permute-done | bytes 131104 | tf_op jit(solution)/shard_map/ppermute | solution.py:16
  43.4 4.0 %fusion.23 = (f32[8,128]{1,0:T(8,128)S(1)}, f32[8,128,512]{1,2,0:T(8,128)}) fusion(pred[128,512]{0,1:T(8,128)(4,1)S(1)} %compare_and_fusion, f32[512,128,8]{1,0,2:T(8,128)S(1)} %fusion.16, bf16[128,8,512]{2,1,0:T(8,128)(2,1)S(1)} %copy-done, bf16[128,512]{1,0:T(8,128)(2,1)} %collective-permute-done.2, bf16[128,512]{1,0:T(8,128)(2,1)} %collective-permute-done.1, ...), kind=kOutput, calls=%fused_computation.43 | convolution fusion | flops 542114304 | bytes 5836800 | tf_op jit(solution)/shard_map/sub | solution.py:51
  47.3 2.7 %convolution_bitcast_fusion = f32[512,512]{1,0:T(8,128)S(1)} fusion(bf16[128,8,512]{0,2,1:T(8,128)(2,1)} %copy.63, f32[8,128,512]{1,2,0:T(8,128)} %get-tuple-element.27, f32[8,128]{1,0:T(8,128)S(1)} %get-tuple-element.26), kind=kOutput, calls=%fused_computation.10 | convolution fusion | flops 537919488 | bytes 4198400 | tf_op jit(solution)/shard_map/hqk,qhd->kd/dot_general | solution.py:71
  50.2 1.9 %fusion.1 = f32[128,8]{0,1:T(8,128)S(1)} fusion(bf16[128,8,512]{0,2,1:T(8,128)(2,1)S(1)} %copy-done.1, bf16[128,512]{1,0:T(8,128)(2,1)} %collective-permute-done.2, bf16[128,512]{1,0:T(8,128)(2,1)} %collective-permute-done.1, bf16[128,512]{1,0:T(8,128)(2,1)} %collective-permute-done, bf16[128,512]{1,0:T(8,128)(2,1)} %param.8, ...), kind=kOutput, calls=%fused_computation.2 | convolution fusion | flops 541588480 | bytes 3678208 | tf_op jit(solution)/shard_map/hqk,kd->qhd/dot_general | solution.py:54
  52.1 1.8 %fusion.3 = bf16[8,128,512]{1,2,0:T(8,128)(2,1)S(1)} fusion(bf16[128,8,512]{0,2,1:T(8,128)(2,1)S(1)} %copy-done.1, f32[8,128]{1,0:T(8,128)S(1)} %bitcast.63, f32[8,128,512]{1,2,0:T(8,128)S(1)} %copy-done.3, f32[8,128]{1,0:T(8,128)S(1)} %get-tuple-element.26, bf16[128,512]{1,0:T(8,128)(2,1)} %collective-permute-done.2, ...), kind=kOutput, calls=%fused_computation.5 | convolution fusion | flops 541065216 | bytes 4726784 | tf_op jit(solution)/shard_map/qhd,kd->hqk/dot_general | solution.py:56
  55.0 1.9 %collective-permute-start.10 = (bf16[128,64]{0,1:T(8,128)(2,1)}, bf16[128,64]{0,1:T(8,128)(2,1)S(1)}, u32[]{:S(2)}, u32[]{:S(2)}) collective-permute-start(bf16[128,64]{0,1:T(8,128)(2,1)} %get-tuple-element.25), channel_id=1, source_target_pairs={{32,0},{48,16},{64,32},{80,48},{96,64},{112,80},{128,96},{144,112}... | collective-permute-start | bytes 49160 | tf_op jit(solution)/shard_map/ppermute | solution.py:16
  56.9 1.9 %collective-permute-start.11 = (bf16[128,64]{0,1:T(8,128)(2,1)S(1)}, bf16[128,64]{0,1:T(8,128)(2,1)S(1)}, u32[]{:S(2)}, u32[]{:S(2)}) collective-permute-start(bf16[128,64]{0,1:T(8,128)(2,1)S(1)} %get-tuple-element.24), channel_id=1, source_target_pairs={{48,0},{64,16},{80,32},{96,48},{112,64},{128,80},{144,96},{160,112... | collective-permute-start | bytes 49160 | tf_op jit(solution)/shard_map/ppermute | solution.py:16
  58.8 0.9 fusion.24
  59.8 3.4 %collective-permute-start.6 = (bf16[128,512]{1,0:T(8,128)(2,1)S(1)}, bf16[128,512]{1,0:T(8,128)(2,1)S(1)}, u32[]{:S(2)}, u32[]{:S(2)}) collective-permute-start(bf16[128,512]{1,0:T(8,128)(2,1)S(1)} %get-tuple-element.20), channel_id=1, source_target_pairs={{16,0},{32,16},{48,32},{64,48},{80,64},{96,80},{112,96},{128,112},... | collective-permute-start | bytes 393224 | tf_op jit(solution)/shard_map/ppermute | solution.py:16
  63.1 1.9 %collective-permute-start.7 = (bf16[128,512]{1,0:T(8,128)(2,1)S(1)}, bf16[128,512]{1,0:T(8,128)(2,1)S(1)}, u32[]{:S(2)}, u32[]{:S(2)}) collective-permute-start(bf16[128,512]{1,0:T(8,128)(2,1)S(1)} %get-tuple-element.22), channel_id=1, source_target_pairs={{32,0},{48,16},{64,32},{80,48},{96,64},{112,80},{128,96},{144,112}... | collective-permute-start | bytes 393224 | tf_op jit(solution)/shard_map/ppermute | solution.py:16
  65.1 2.6 %collective-permute-start.8 = (bf16[128,512]{1,0:T(8,128)(2,1)S(1)}, bf16[128,512]{1,0:T(8,128)(2,1)S(1)}, u32[]{:S(2)}, u32[]{:S(2)}) collective-permute-start(bf16[128,512]{1,0:T(8,128)(2,1)S(1)} %get-tuple-element.21), channel_id=1, source_target_pairs={{48,0},{64,16},{80,32},{96,48},{112,64},{128,80},{144,96},{160,112... | collective-permute-start | bytes 393224 | tf_op jit(solution)/shard_map/ppermute | solution.py:16
  67.6 1.8 %fusion.4 = bf16[128,8,512]{0,2,1:T(8,128)(2,1)S(1)} fusion(bf16[8,128,512]{1,2,0:T(8,128)(2,1)S(1)} %fusion.3, bf16[128,512]{1,0:T(8,128)(2,1)} %collective-permute-done.2, bf16[128,512]{1,0:T(8,128)(2,1)} %collective-permute-done.1, bf16[128,512]{1,0:T(8,128)(2,1)} %collective-permute-done, bf16[128,512]{1,0:T(8,128)(2,1)} %param.8), kind=kOutput, calls=%fused_computation.9 | convolution fusion | flops 540016640 | bytes 2621440 | tf_op jit(solution)/shard_map/hqk,kd->qhd/dot_general | solution.py:62
  69.5 2.5 %collective-permute-start.9 = (bf16[128,64]{0,1:T(8,128)(2,1)S(1)}, bf16[128,64]{0,1:T(8,128)(2,1)S(1)}, u32[]{:S(2)}, u32[]{:S(2)}) collective-permute-start(bf16[128,64]{0,1:T(8,128)(2,1)S(1)} %get-tuple-element.23), channel_id=1, source_target_pairs={{16,0},{32,16},{48,32},{64,48},{80,64},{96,80},{112,96},{128,112},... | collective-permute-start | bytes 49160 | tf_op jit(solution)/shard_map/ppermute | solution.py:16
  72.0 1.3 collective-permute-done.8
  73.3 0.7 fusion.13
  74.4 1.7 %copy.72 = bf16[128,8,512]{2,1,0:T(8,128)(2,1)} copy(bf16[128,8,512]{0,2,1:T(8,128)(2,1)S(1)} %fusion.4) | data formatting | bytes 2097152
  76.1 0.8 copy.73
  76.9 68.8 %all-reduce = bf16[128,64]{0,1:T(8,128)(2,1)S(1)} all-reduce(f32[128,64]{0,1:T(8,128)S(1)} %fusion.15), channel_id=3, replica_groups=mesh['tok'=64,'head'=16] {'head'}, use_global_device_ids=true, to_apply=%region_6.7.clone | all-reduce | flops 8192 | bytes 49152
  145.8 0.7 copy.74
  146.5 10.0 %reduce-scatter.3.cloned.1.call-done = f32[8,512]{1,0:T(8,128)} async-done(((f32[128,512]{1,0:T(8,128)}), f32[8,512]{1,0:T(8,128)}) %reduce-scatter.3.cloned.1.call-update) | async-done | bytes 16400 | tf_op jit(solution)/shard_map/reduce_scatter | solution.py:87
  156.5 1.3 convert_element_type.65
  (35 shorter events, 2.6 us)
Async XLA Ops:
  7.2 36.2 %copy-start = (bf16[128,8,512]{2,1,0:T(8,128)(2,1)S(1)}, bf16[128,8,512]{2,1,0:T(8,128)(2,1)}, u32[]{:S(2)}) copy-start(bf16[128,8,512]{2,1,0:T(8,128)(2,1)} %param.6) | copy-start | bytes 3145732
  7.2 27.0 %copy-start.2 = (bf16[128,64]{0,1:T(8,128)(2,1)S(1)}, bf16[128,64]{0,1:T(8,128)(2,1)}, u32[]{:S(2)}) copy-start(bf16[128,64]{0,1:T(8,128)(2,1)} %param.9) | copy-start | bytes 49156
  7.2 149.3 %reduce-scatter.3.cloned.1.call-start = ((), (), s32[]{:S(2)}) async-start(), calls=%async_computation.1 | async-start | bytes 278528 | tf_op jit(solution)/shard_map/reduce_scatter | solution.py:87
  7.2 24.3 %collective-permute-start.3 = (bf16[128,64]{0,1:T(8,128)(2,1)}, bf16[128,64]{0,1:T(8,128)(2,1)S(1)}, u32[]{:S(2)}, u32[]{:S(2)}) collective-permute-start(bf16[128,64]{0,1:T(8,128)(2,1)} %param.9), channel_id=1, source_target_pairs={{0,16},{16,32},{32,48},{48,64},{64,80},{80,96},{96,112},{112,128},... | collective-permute-start | bytes 49160 | tf_op jit(solution)/shard_map/ppermute | solution.py:16
  9.3 24.8 %collective-permute-start.4 = (bf16[128,64]{0,1:T(8,128)(2,1)}, bf16[128,64]{0,1:T(8,128)(2,1)S(1)}, u32[]{:S(2)}, u32[]{:S(2)}) collective-permute-start(bf16[128,64]{0,1:T(8,128)(2,1)} %param.9), channel_id=1, source_target_pairs={{0,32},{16,48},{32,64},{48,80},{64,96},{80,112},{96,128},{112,144}... | collective-permute-start | bytes 49160 | tf_op jit(solution)/shard_map/ppermute | solution.py:16
  12.8 21.4 %collective-permute-start.5 = (bf16[128,64]{0,1:T(8,128)(2,1)}, bf16[128,64]{0,1:T(8,128)(2,1)S(1)}, u32[]{:S(2)}, u32[]{:S(2)}) collective-permute-start(bf16[128,64]{0,1:T(8,128)(2,1)} %param.9), channel_id=1, source_target_pairs={{0,48},{16,64},{32,80},{48,96},{64,112},{80,128},{96,144},{112,160... | collective-permute-start | bytes 49160 | tf_op jit(solution)/shard_map/ppermute | solution.py:16
  17.3 17.3 %collective-permute-start = (bf16[128,512]{1,0:T(8,128)(2,1)}, bf16[128,512]{1,0:T(8,128)(2,1)}, u32[]{:S(2)}, u32[]{:S(2)}) collective-permute-start(bf16[128,512]{1,0:T(8,128)(2,1)} %param.8), channel_id=1, source_target_pairs={{0,16},{16,32},{32,48},{48,64},{64,80},{80,96},{96,112},{112,128},... | collective-permute-start | bytes 393224 | tf_op jit(solution)/shard_map/ppermute | solution.py:16
  19.3 15.3 %collective-permute-start.1 = (bf16[128,512]{1,0:T(8,128)(2,1)}, bf16[128,512]{1,0:T(8,128)(2,1)}, u32[]{:S(2)}, u32[]{:S(2)}) collective-permute-start(bf16[128,512]{1,0:T(8,128)(2,1)} %param.8), channel_id=1, source_target_pairs={{0,32},{16,48},{32,64},{48,80},{64,96},{80,112},{96,128},{112,144}... | collective-permute-start | bytes 393224 | tf_op jit(solution)/shard_map/ppermute | solution.py:16
  31.5 11.8 %collective-permute-start.2 = (bf16[128,512]{1,0:T(8,128)(2,1)}, bf16[128,512]{1,0:T(8,128)(2,1)}, u32[]{:S(2)}, u32[]{:S(2)}) collective-permute-start(bf16[128,512]{1,0:T(8,128)(2,1)} %param.8), channel_id=1, source_target_pairs={{0,48},{16,64},{32,80},{48,96},{64,112},{80,128},{96,144},{112,160... | collective-permute-start | bytes 393224 | tf_op jit(solution)/shard_map/ppermute | solution.py:16
  47.3 2.8 %copy-start.1 = (bf16[128,8,512]{0,2,1:T(8,128)(2,1)S(1)}, bf16[128,8,512]{0,2,1:T(8,128)(2,1)}, u32[]{:S(2)}) copy-start(bf16[128,8,512]{0,2,1:T(8,128)(2,1)} %copy.63) | copy-start | bytes 3145732
  47.3 2.9 %copy-start.3 = (f32[8,128,512]{1,2,0:T(8,128)S(1)}, f32[8,128,512]{1,2,0:T(8,128)}, u32[]{:S(2)}) copy-start(f32[8,128,512]{1,2,0:T(8,128)} %get-tuple-element.27) | copy-start | bytes 6291460
  55.0 21.9 %collective-permute-start.10 = (bf16[128,64]{0,1:T(8,128)(2,1)}, bf16[128,64]{0,1:T(8,128)(2,1)S(1)}, u32[]{:S(2)}, u32[]{:S(2)}) collective-permute-start(bf16[128,64]{0,1:T(8,128)(2,1)} %get-tuple-element.25), channel_id=1, source_target_pairs={{32,0},{48,16},{64,32},{80,48},{96,64},{112,80},{128,96},{144,112}... | collective-permute-start | bytes 49160 | tf_op jit(solution)/shard_map/ppermute | solution.py:16
  56.9 19.9 %collective-permute-start.11 = (bf16[128,64]{0,1:T(8,128)(2,1)S(1)}, bf16[128,64]{0,1:T(8,128)(2,1)S(1)}, u32[]{:S(2)}, u32[]{:S(2)}) collective-permute-start(bf16[128,64]{0,1:T(8,128)(2,1)S(1)} %get-tuple-element.24), channel_id=1, source_target_pairs={{48,0},{64,16},{80,32},{96,48},{112,64},{128,80},{144,96},{160,112... | collective-permute-start | bytes 49160 | tf_op jit(solution)/shard_map/ppermute | solution.py:16
  59.8 9.7 %collective-permute-start.6 = (bf16[128,512]{1,0:T(8,128)(2,1)S(1)}, bf16[128,512]{1,0:T(8,128)(2,1)S(1)}, u32[]{:S(2)}, u32[]{:S(2)}) collective-permute-start(bf16[128,512]{1,0:T(8,128)(2,1)S(1)} %get-tuple-element.20), channel_id=1, source_target_pairs={{16,0},{32,16},{48,32},{64,48},{80,64},{96,80},{112,96},{128,112},... | collective-permute-start | bytes 393224 | tf_op jit(solution)/shard_map/ppermute | solution.py:16
  63.1 8.8 %collective-permute-start.7 = (bf16[128,512]{1,0:T(8,128)(2,1)S(1)}, bf16[128,512]{1,0:T(8,128)(2,1)S(1)}, u32[]{:S(2)}, u32[]{:S(2)}) collective-permute-start(bf16[128,512]{1,0:T(8,128)(2,1)S(1)} %get-tuple-element.22), channel_id=1, source_target_pairs={{32,0},{48,16},{64,32},{80,48},{96,64},{112,80},{128,96},{144,112}... | collective-permute-start | bytes 393224 | tf_op jit(solution)/shard_map/ppermute | solution.py:16
  65.1 8.2 %collective-permute-start.8 = (bf16[128,512]{1,0:T(8,128)(2,1)S(1)}, bf16[128,512]{1,0:T(8,128)(2,1)S(1)}, u32[]{:S(2)}, u32[]{:S(2)}) collective-permute-start(bf16[128,512]{1,0:T(8,128)(2,1)S(1)} %get-tuple-element.21), channel_id=1, source_target_pairs={{48,0},{64,16},{80,32},{96,48},{112,64},{128,80},{144,96},{160,112... | collective-permute-start | bytes 393224 | tf_op jit(solution)/shard_map/ppermute | solution.py:16
  69.5 7.4 %collective-permute-start.9 = (bf16[128,64]{0,1:T(8,128)(2,1)S(1)}, bf16[128,64]{0,1:T(8,128)(2,1)S(1)}, u32[]{:S(2)}, u32[]{:S(2)}) collective-permute-start(bf16[128,64]{0,1:T(8,128)(2,1)S(1)} %get-tuple-element.23), channel_id=1, source_target_pairs={{16,0},{32,16},{48,32},{64,48},{80,64},{96,80},{112,96},{128,112},... | collective-permute-start | bytes 49160 | tf_op jit(solution)/shard_map/ppermute | solution.py:16
Sparse Core Ops, SparseCore 0:
  74.2 82.2 reduce-scatter.2
where the time goes:
time: 165 us
  blocking collectives  68.8 us (42%)
  starting transfers between devices  33.5 us (20%)
  waiting for transfers between devices  20.1 us (12%)
  between operations  15 us (9%)
  matrix products  14.3 us (9%)
  local copies, waits for them, and re-layouts  9.66 us (6%)
  other arithmetic  3.16 us (2%)
    unnamed x1, blocking collectives  68.8 us
    ppermute x12, starting transfers between devices, shifted(): return lax.ppermute(block, axis, route)  33.5 us
    ppermute x12, waiting for transfers between devices, shifted(): return lax.ppermute(block, axis, route)  10.1 us
    reduce_scatter x1, waiting for transfers between devices, body(): lax.psum_scatter(total_latent, 'head', scatter_dimension=0, tiled=True)  10 us
    unnamed x14, local copies, waits for them, and re-layouts  8.19 us
    sub x1, matrix products, body(): exp_terms = jnp.where(visible[None], jnp.exp(masked - row_max), 0.0)  3.96 us
  transfers between devices with their start and end apart: 13, of which 3 were waited for; matrix products, arithmetic and copies ran while one was open for 9% of the time, Pallas kernels for 0%

commit v1 on v0

v1 whole, which is shorter than its diff:
```python
import jax
import jax.numpy as jnp
from jax import lax
from jax.sharding import PartitionSpec as P

SPAN = 3


SCALE = 0.07216878364870322
NEGATIVE = -1e30


def shifted(block, axis, distance):
    devices = range(lax.axis_size(axis))
    route = [(i - distance, i) for i in devices if i - distance in devices]
    return lax.ppermute(block, axis, route)


def body(query_latent, query_rotary, latents, key_rotary, out_grad, doc_lengths):
    tok_rows, latent_width = latents.shape
    head_count = query_latent.shape[1]
    rotary_width = key_rotary.shape[1]
    head_devices = lax.axis_size("head")
    shard = lax.axis_index("tok")
    offsets = jnp.arange(tok_rows, dtype=jnp.int32)
    query_pos = shard * tok_rows + offsets
    doc_starts = jnp.cumsum(doc_lengths) - doc_lengths
    query_start = jnp.max(
        jnp.where(doc_starts[None, :] <= query_pos[:, None], doc_starts[None, :], 0), axis=1
    )
    own_keys = jnp.concatenate([latents, key_rotary], axis=1)
    key_tiles = [own_keys]
    place_tiles = [query_pos]
    for distance in range(1, SPAN + 1):
        key_tiles.append(shifted(own_keys, "tok", distance))
        place_tiles.append(query_pos - distance * tok_rows)
    keys = jnp.concatenate(key_tiles, axis=0)
    key_latent = keys[:, :latent_width]
    key_rot = keys[:, latent_width:]
    key_place = jnp.concatenate(place_tiles, axis=0)
    rotary_query = query_rotary.reshape(tok_rows, head_count, rotary_width)
    visible = (key_place[None, :] >= query_start[:, None]) & (
        key_place[None, :] <= query_pos[:, None]
    )
    scores = SCALE * (
        jnp.einsum("qhd,kd->hqk", query_latent, key_latent, preferred_element_type=jnp.float32)
        + jnp.einsum("qhr,kr->hqk", rotary_query, key_rot, preferred_element_type=jnp.float32)
    )
    masked = jnp.where(visible[None], scores, NEGATIVE)
    row_max = jnp.max(masked, axis=2, keepdims=True)
    exp_terms = jnp.where(visible[None], jnp.exp(masked - row_max), 0.0)
    attn_probs = exp_terms / jnp.sum(exp_terms, axis=2, keepdims=True)
    probs_low = attn_probs.astype(jnp.bfloat16)
    prob_grad = jnp.einsum("qhd,kd->hqk", out_grad, key_latent, preferred_element_type=jnp.float32)
    row_delta = jnp.sum(probs_low.astype(jnp.float32) * prob_grad, axis=2, keepdims=True)
    score_grad = (attn_probs * (prob_grad - row_delta)).astype(jnp.bfloat16)
    grad_query_latent = (
        SCALE
        * jnp.einsum("hqk,kd->qhd", score_grad, key_latent, preferred_element_type=jnp.float32)
    ).astype(jnp.bfloat16)
    grad_query_rotary = (
        (SCALE * jnp.einsum("hqk,kr->qhr", score_grad, key_rot, preferred_element_type=jnp.float32))
        .reshape(tok_rows, head_count * rotary_width)
        .astype(jnp.bfloat16)
    )
    latent_grad = SCALE * jnp.einsum(
        "hqk,qhd->kd", score_grad, query_latent, preferred_element_type=jnp.float32
    ) + jnp.einsum("hqk,qhd->kd", probs_low, out_grad, preferred_element_type=jnp.float32)
    rotary_grad = SCALE * jnp.einsum(
        "hqk,qhr->kr", score_grad, rotary_query, preferred_element_type=jnp.float32
    )
    key_grad = jnp.concatenate([latent_grad, rotary_grad], axis=1)
    total = key_grad[:tok_rows]
    for distance in range(1, SPAN + 1):
        piece = key_grad[distance * tok_rows : (distance + 1) * tok_rows].astype(jnp.bfloat16)
        total = total + shifted(piece, "tok", -distance).astype(jnp.float32)
    blocks = total.astype(jnp.bfloat16).reshape(head_devices, tok_rows // head_devices, -1)
    blocks = lax.all_to_all(blocks, "head", split_axis=0, concat_axis=0, tiled=True)
    summed = jnp.sum(blocks.astype(jnp.float32), axis=0).astype(jnp.bfloat16)
    return (
        grad_query_latent,
        grad_query_rotary,
        summed[:, :latent_width],
        summed[:, latent_width:],
    )


def solution(mesh):
    in_specs = (
        P("tok", "head", None),
        P("tok", "head"),
        P("tok", None),
        P("tok", None),
        P("tok", "head", None),
        P(),
    )
    out_specs = (
        P("tok", "head", None),
        P("tok", "head"),
        P(("tok", "head"), None),
        P(("tok", "head"), None),
    )
    return jax.shard_map(body, mesh=mesh, in_specs=in_specs, out_specs=out_specs, check_vma=False)
```

time: 165 us -> 83.2 us (0.50)
  the two profiles are of different devices: /device:TPU:2 before, /device:TPU:57 now
where the time goes in v1:
time: 83.2 us; the launch traced here: 81.8 us
  starting transfers between devices  36.4 us (44%)
  waiting for transfers between devices  18 us (22%)
  local copies, waits for them, and re-layouts  10.9 us (13%)
  matrix products  10.6 us (13%)
  other arithmetic  5.02 us (6%)
  between operations  0.92 us (1%)
    all_to_all x1, starting transfers between devices, body(): lax.all_to_all(blocks, 'head', split_axis=0, concat_axis=0, tiled=True)  18.6 us
    ppermute x6, starting transfers between devices, shifted(): return lax.ppermute(block, axis, route)  17.8 us
    all_to_all x1, waiting for transfers between devices, body(): lax.all_to_all(blocks, 'head', split_axis=0, concat_axis=0, tiled=True)  10.4 us
    unnamed x16, local copies, waits for them, and re-layouts  8.1 us
    ppermute x6, waiting for transfers between devices, shifted(): return lax.ppermute(block, axis, route)  7.59 us
    sub x1, matrix products, body(): exp_terms = jnp.where(visible[None], jnp.exp(masked - row_max), 0.0)  2.96 us
    dot_general x1, matrix products, body(): jnp.einsum('qhd,kd->hqk', out_grad, key_latent, preferred_element_type=jn...  2.88 us
    convert_element_type x1, other arithmetic, body(): score_grad = (attn_probs * (prob_grad - row_delta)).astype(jnp.bfloat16)  1.89 us
  transfers between devices with their start and end apart: 7, of which 4 were waited for; matrix products, arithmetic and copies ran while one was open for 12% of the time, Pallas kernels for 0%

profile of v1, /device:TPU:57, one launch (start us, length us, event | category | flops | bytes accessed | tf_op | source)
XLA Modules:
  0.0 81.8 jit_solution(10390895354489213142)
XLA Ops:
  0.6 0.9 %copy.46 = bf16[128,64]{1,0:T(8,128)(2,1)S(1)} copy(bf16[128,64]{0,1:T(8,128)(2,1)} %param.9) | data formatting | bytes 32768 | tf_op args[3]
  1.6 0.9 %pad_maximum_fusion.2 = bf16[128,576]{1,0:T(8,128)(2,1)S(1)} fusion(bf16[128,64]{1,0:T(8,128)(2,1)S(1)} %copy.46, bf16[128,512]{1,0:T(8,128)(2,1)} %param.8), kind=kLoop, calls=%fused_computation.33 | loop fusion | flops 294912 | bytes 294912 | tf_op jit(solution)/shard_map/concatenate | solution.py:31
  2.5 3.9 %collective-permute-start.2 = (bf16[128,576]{1,0:T(8,128)(2,1)S(1)}, bf16[128,576]{1,0:T(8,128)(2,1)S(1)}, u32[]{:S(2)}, u32[]{:S(2)}) collective-permute-start(bf16[128,576]{1,0:T(8,128)(2,1)S(1)} %pad_maximum_fusion.2), channel_id=1, source_target_pairs={{0,48},{16,64},{32,80},{48,96},{64,112},{80,128},{96,144},{112,160... | collective-permute-start | bytes 442376 | tf_op jit(solution)/shard_map/ppermute | solution.py:16
  6.4 3.2 %collective-permute-start.1 = (bf16[128,576]{1,0:T(8,128)(2,1)S(1)}, bf16[128,576]{1,0:T(8,128)(2,1)S(1)}, u32[]{:S(2)}, u32[]{:S(2)}) collective-permute-start(bf16[128,576]{1,0:T(8,128)(2,1)S(1)} %pad_maximum_fusion.2), channel_id=1, source_target_pairs={{0,32},{16,48},{32,64},{48,80},{64,96},{80,112},{96,128},{112,144}... | collective-permute-start | bytes 442376 | tf_op jit(solution)/shard_map/ppermute | solution.py:16
  9.6 2.2 %collective-permute-start = (bf16[128,576]{1,0:T(8,128)(2,1)S(1)}, bf16[128,576]{1,0:T(8,128)(2,1)S(1)}, u32[]{:S(2)}, u32[]{:S(2)}) collective-permute-start(bf16[128,576]{1,0:T(8,128)(2,1)S(1)} %pad_maximum_fusion.2), channel_id=1, source_target_pairs={{0,16},{16,32},{32,48},{48,64},{64,80},{80,96},{96,112},{112,128},... | collective-permute-start | bytes 442376 | tf_op jit(solution)/shard_map/ppermute | solution.py:16
  11.8 0.8 copy.47
  12.8 0.7 sub.34
  13.4 1.0 %copy.49 = bf16[128,512]{0,1:T(8,128)(2,1)S(1)} copy(bf16[128,512]{1,0:T(8,128)(2,1)} %param.7) | data formatting | bytes 262144 | tf_op args[1]
  14.5 2.0 %copy.57 = bf16[128,8,512]{0,2,1:T(8,128)(2,1)S(1)} copy(bf16[128,8,512]{2,1,0:T(8,128)(2,1)} %param.6) | data formatting | bytes 2097152 | tf_op args[0]
  16.5 1.7 %copy.59 = bf16[128,8,512]{0,2,1:T(8,128)(2,1)} copy(bf16[128,8,512]{2,1,0:T(8,128)(2,1)S(1)} %copy-done.2) | data formatting | bytes 2097152 | tf_op args[4]
  18.5 1.8 %fusion.20 = f32[512,128,8]{1,0,2:T(8,128)} fusion(bf16[512,64,1]{1,0,2:T(8,128)(2,1)S(1)} %maximum_bitcast_fusion, bf16[128,8,64]{0,2,1:T(8,128)(2,1)S(1)} %bitcast.58), kind=kOutput, calls=%fused_computation.43 | convolution fusion | flops 67108864 | bytes 2293760 | tf_op jit(solution)/shard_map/qhr,kr->hqk/dot_general | solution.py:47
  20.3 0.9 %pad_maximum_fusion.1 = bf16[512,576]{1,0:T(8,128)(2,1)} fusion(bf16[128,576]{1,0:T(8,128)(2,1)S(1)} %collective-permute-done.2, bf16[128,576]{1,0:T(8,128)(2,1)S(1)} %collective-permute-done.1, bf16[128,576]{1,0:T(8,128)(2,1)S(1)} %collective-permute-done, bf16[128,64]{1,0:T(8,128)(2,1)S(1)} %copy.46, bf16[128,512]{1,0:T(8,128)(2,1)S(1)} %copy-done.1), kind=kLoop, calls=%fused_computation.24 | loop fusion | flops 2949120 | bytes 1179648 | tf_op jit(solution)/shard_map/concatenate | solution.py:37
  21.2 3.0 %fusion.19 = (f32[8,128]{1,0:T(8,128)S(1)}, f32[8,128,512]{1,2,0:T(8,128)S(1)}) fusion(pred[128,512]{0,1:T(8,128)(4,1)S(1)} %compare_and_fusion, f32[512,128,8]{1,0,2:T(8,128)} %fusion.20, bf16[128,8,512]{0,2,1:T(8,128)(2,1)S(1)} %copy.57, bf16[512,576]{1,0:T(8,128)(2,1)} %pad_maximum_fusion.1), kind=kOutput, calls=%fused_computation.42 | convolution fusion | flops 540017152 | bytes 5902336 | tf_op jit(solution)/shard_map/sub | solution.py:51
  24.1 2.9 %fusion.1 = (f32[8,128]{1,0:T(8,128)S(1)}, f32[512,128,8]{1,0,2:T(8,128)S(1)}) fusion(f32[8,128,512]{1,2,0:T(8,128)S(1)} %get-tuple-element.20, f32[8,128]{1,0:T(8,128)S(1)} %get-tuple-element.19, bf16[128,8,512]{0,2,1:T(8,128)(2,1)} %copy.59, bf16[512,576]{1,0:T(8,128)(2,1)} %pad_maximum_fusion.1), kind=kOutput, calls=%fused_computation.3 | convolution fusion | flops 539491328 | bytes 5775360 | tf_op jit(solution)/shard_map/qhd,kd->hqk/dot_general | solution.py:54
  27.1 0.7 convolution_bitcast_fusion
  27.8 1.9 %fusion.3 = bf16[8,128,512]{1,2,0:T(8,128)(2,1)S(1)} fusion(f32[512,128,8]{1,0,2:T(8,128)S(1)} %get-tuple-element.22, f32[8,128]{1,0:T(8,128)S(1)} %get-tuple-element.21, f32[8,128,512]{1,2,0:T(8,128)} %copy-done, f32[8,128]{1,0:T(8,128)S(1)} %get-tuple-element.19), kind=kLoop, calls=%fused_computation.5 | loop fusion | flops 2097152 | bytes 5251072 | tf_op jit(solution)/shard_map/convert_element_type | solution.py:56
  29.7 0.4 fusion.9
  30.1 0.7 fusion.6
  31.1 3.1 %collective-permute-start.5 = (bf16[128,576]{0,1:T(8,128)(2,1)S(1)}, bf16[128,576]{0,1:T(8,128)(2,1)S(1)}, u32[]{:S(2)}, u32[]{:S(2)}) collective-permute-start(bf16[128,576]{0,1:T(8,128)(2,1)S(1)} %get-tuple-element.17), channel_id=1, source_target_pairs={{48,0},{64,16},{80,32},{96,48},{112,64},{128,80},{144,96},{160,112... | collective-permute-start | bytes 442376 | tf_op jit(solution)/shard_map/ppermute | solution.py:16
  34.2 3.0 %collective-permute-start.4 = (bf16[128,576]{0,1:T(8,128)(2,1)S(1)}, bf16[128,576]{0,1:T(8,128)(2,1)S(1)}, u32[]{:S(2)}, u32[]{:S(2)}) collective-permute-start(bf16[128,576]{0,1:T(8,128)(2,1)S(1)} %get-tuple-element.18), channel_id=1, source_target_pairs={{32,0},{48,16},{64,32},{80,48},{96,64},{112,80},{128,96},{144,112}... | collective-permute-start | bytes 442376 | tf_op jit(solution)/shard_map/ppermute | solution.py:16
  37.2 2.4 %collective-permute-start.3 = (bf16[128,576]{0,1:T(8,128)(2,1)S(1)}, bf16[128,576]{0,1:T(8,128)(2,1)S(1)}, u32[]{:S(2)}, u32[]{:S(2)}) collective-permute-start(bf16[128,576]{0,1:T(8,128)(2,1)S(1)} %get-tuple-element.16), channel_id=1, source_target_pairs={{16,0},{32,16},{48,32},{64,48},{80,64},{96,80},{112,96},{128,112},... | collective-permute-start | bytes 442376 | tf_op jit(solution)/shard_map/ppermute | solution.py:16
  39.6 3.3 %collective-permute-done.5 = bf16[128,576]{0,1:T(8,128)(2,1)S(1)} collective-permute-done((bf16[128,576]{0,1:T(8,128)(2,1)S(1)}, bf16[128,576]{0,1:T(8,128)(2,1)S(1)}, u32[]{:S(2)}, u32[]{:S(2)}) %collective-permute-start.5) | collective-permute-done | bytes 147488 | tf_op jit(solution)/shard_map/ppermute | solution.py:16
  42.9 2.6 %collective-permute-done.4 = bf16[128,576]{0,1:T(8,128)(2,1)S(1)} collective-permute-done((bf16[128,576]{0,1:T(8,128)(2,1)S(1)}, bf16[128,576]{0,1:T(8,128)(2,1)S(1)}, u32[]{:S(2)}, u32[]{:S(2)}) %collective-permute-start.4) | collective-permute-done | bytes 147488 | tf_op jit(solution)/shard_map/ppermute | solution.py:16
  45.6 1.6 %collective-permute-done.3 = bf16[128,576]{0,1:T(8,128)(2,1)S(1)} collective-permute-done((bf16[128,576]{0,1:T(8,128)(2,1)S(1)}, bf16[128,576]{0,1:T(8,128)(2,1)S(1)}, u32[]{:S(2)}, u32[]{:S(2)}) %collective-permute-start.3) | collective-permute-done | bytes 147488 | tf_op jit(solution)/shard_map/ppermute | solution.py:16
  47.3 0.8 copy.61
  48.1 18.6 %all-to-all-start = ((bf16[16,8,576]{2,1,0:T(8,128)(2,1)}), bf16[16,8,576]{2,1,0:T(8,128)(2,1)S(1)}, u32[]{:S(2)}, u32[]{:S(2)}) async-start(bf16[16,8,576]{2,1,0:T(8,128)(2,1)} %bitcast.14), calls=%async_computation | async-start | bytes 327680 | tf_op jit(solution)/shard_map/all_to_all | solution.py:78
  66.7 0.7 fusion.4
  67.4 1.7 %copy.62 = bf16[128,8,512]{2,1,0:T(8,128)(2,1)} copy(bf16[128,8,512]{0,2,1:T(8,128)(2,1)S(1)} %fusion.4) | data formatting | bytes 2097152
  69.4 0.8 copy.63
  70.2 10.4 %all-to-all-done = bf16[16,8,576]{2,1,0:T(8,128)(2,1)S(1)} async-done(((bf16[16,8,576]{2,1,0:T(8,128)(2,1)}), bf16[16,8,576]{2,1,0:T(8,128)(2,1)S(1)}, u32[]{:S(2)}, u32[]{:S(2)}) %all-to-all-start) | async-done | bytes 147488 | tf_op jit(solution)/shard_map/all_to_all | solution.py:78
  80.7 0.6 slice.41
  81.3 0.6 slice.42
  (27 shorter events, 1.1 us)
Async XLA Ops:
  0.6 15.8 %copy-start.2 = (bf16[128,8,512]{2,1,0:T(8,128)(2,1)S(1)}, bf16[128,8,512]{2,1,0:T(8,128)(2,1)}, u32[]{:S(2)}) copy-start(bf16[128,8,512]{2,1,0:T(8,128)(2,1)} %param.10) | copy-start | bytes 3145732
  2.5 15.9 %collective-permute-start.2 = (bf16[128,576]{1,0:T(8,128)(2,1)S(1)}, bf16[128,576]{1,0:T(8,128)(2,1)S(1)}, u32[]{:S(2)}, u32[]{:S(2)}) collective-permute-start(bf16[128,576]{1,0:T(8,128)(2,1)S(1)} %pad_maximum_fusion.2), channel_id=1, source_target_pairs={{0,48},{16,64},{32,80},{48,96},{64,112},{80,128},{96,144},{112,160... | collective-permute-start | bytes 442376 | tf_op jit(solution)/shard_map/ppermute | solution.py:16
  6.4 12.0 %collective-permute-start.1 = (bf16[128,576]{1,0:T(8,128)(2,1)S(1)}, bf16[128,576]{1,0:T(8,128)(2,1)S(1)}, u32[]{:S(2)}, u32[]{:S(2)}) collective-permute-start(bf16[128,576]{1,0:T(8,128)(2,1)S(1)} %pad_maximum_fusion.2), channel_id=1, source_target_pairs={{0,32},{16,48},{32,64},{48,80},{64,96},{80,112},{96,128},{112,144}... | collective-permute-start | bytes 442376 | tf_op jit(solution)/shard_map/ppermute | solution.py:16
  9.6 8.8 %collective-permute-start = (bf16[128,576]{1,0:T(8,128)(2,1)S(1)}, bf16[128,576]{1,0:T(8,128)(2,1)S(1)}, u32[]{:S(2)}, u32[]{:S(2)}) collective-permute-start(bf16[128,576]{1,0:T(8,128)(2,1)S(1)} %pad_maximum_fusion.2), channel_id=1, source_target_pairs={{0,16},{16,32},{32,48},{48,64},{64,80},{80,96},{96,112},{112,128},... | collective-permute-start | bytes 442376 | tf_op jit(solution)/shard_map/ppermute | solution.py:16
  14.5 4.0 %copy-start.1 = (bf16[128,512]{1,0:T(8,128)(2,1)S(1)}, bf16[128,512]{1,0:T(8,128)(2,1)}, u32[]{:S(2)}) copy-start(bf16[128,512]{1,0:T(8,128)(2,1)} %param.8) | copy-start | bytes 393220
  24.1 2.9 %copy-start = (f32[8,128,512]{1,2,0:T(8,128)}, f32[8,128,512]{1,2,0:T(8,128)S(1)}, u32[]{:S(2)}) copy-start(f32[8,128,512]{1,2,0:T(8,128)S(1)} %get-tuple-element.20) | copy-start | bytes 6291460
  24.1 2.9 %copy-start.3 = (bf16[128,8,512]{0,2,1:T(8,128)(2,1)S(1)}, bf16[128,8,512]{0,2,1:T(8,128)(2,1)}, u32[]{:S(2)}) copy-start(bf16[128,8,512]{0,2,1:T(8,128)(2,1)} %copy.59) | copy-start | bytes 3145732
  30.9 35.8 %copy-start.4 = (bf16[512,576]{1,0:T(8,128)(2,1)S(1)}, bf16[512,576]{1,0:T(8,128)(2,1)}, u32[]{:S(2)}) copy-start(bf16[512,576]{1,0:T(8,128)(2,1)} %pad_maximum_fusion.1) | copy-start | bytes 1769476
  31.1 11.9 %collective-permute-start.5 = (bf16[128,576]{0,1:T(8,128)(2,1)S(1)}, bf16[128,576]{0,1:T(8,128)(2,1)S(1)}, u32[]{:S(2)}, u32[]{:S(2)}) collective-permute-start(bf16[128,576]{0,1:T(8,128)(2,1)S(1)} %get-tuple-element.17), channel_id=1, source_target_pairs={{48,0},{64,16},{80,32},{96,48},{112,64},{128,80},{144,96},{160,112... | collective-permute-start | bytes 442376 | tf_op jit(solution)/shard_map/ppermute | solution.py:16
  34.2 11.4 %collective-permute-start.4 = (bf16[128,576]{0,1:T(8,128)(2,1)S(1)}, bf16[128,576]{0,1:T(8,128)(2,1)S(1)}, u32[]{:S(2)}, u32[]{:S(2)}) collective-permute-start(bf16[128,576]{0,1:T(8,128)(2,1)S(1)} %get-tuple-element.18), channel_id=1, source_target_pairs={{32,0},{48,16},{64,32},{80,48},{96,64},{112,80},{128,96},{144,112}... | collective-permute-start | bytes 442376 | tf_op jit(solution)/shard_map/ppermute | solution.py:16
  37.2 10.0 %collective-permute-start.3 = (bf16[128,576]{0,1:T(8,128)(2,1)S(1)}, bf16[128,576]{0,1:T(8,128)(2,1)S(1)}, u32[]{:S(2)}, u32[]{:S(2)}) collective-permute-start(bf16[128,576]{0,1:T(8,128)(2,1)S(1)} %get-tuple-element.16), channel_id=1, source_target_pairs={{16,0},{32,16},{48,32},{64,48},{80,64},{96,80},{112,96},{128,112},... | collective-permute-start | bytes 442376 | tf_op jit(solution)/shard_map/ppermute | solution.py:16
  48.1 32.5 %all-to-all-start = ((bf16[16,8,576]{2,1,0:T(8,128)(2,1)}), bf16[16,8,576]{2,1,0:T(8,128)(2,1)S(1)}, u32[]{:S(2)}, u32[]{:S(2)}) async-start(bf16[16,8,576]{2,1,0:T(8,128)(2,1)} %bitcast.14), calls=%async_computation | async-start | bytes 327680 | tf_op jit(solution)/shard_map/all_to_all | solution.py:78

commit v2 on v1

v2 whole, which is shorter than its diff:
```python
import jax
import jax.numpy as jnp
from jax import lax
from jax.experimental import pallas as pl
from jax.experimental.pallas import tpu as pltpu
from jax.sharding import PartitionSpec as P

SPAN = 3


SCALE = 0.07216878364870322
LOG2_E = 1.4426950408889634
NEGATIVE = -1e30

TOK = 128
HEADS = 8
DL = 512
DR = 64
ROWS = TOK * HEADS
KEYS = (SPAN + 1) * TOK
FAR = SPAN * TOK
PACK = TOK + TOK * DR // DL
CHUNK = 256
HALF = KEYS // 2

F32 = jnp.float32
BF16 = jnp.bfloat16
VMEM = pltpu.MemorySpace.VMEM
SMEM = pltpu.MemorySpace.SMEM
HBM = pltpu.MemorySpace.HBM

NT = (((1,), (1,)), ((), ()))
NN = (((1,), (0,)), ((), ()))


def dot(a, b, dims):
    return lax.dot_general(a, b, dims, preferred_element_type=F32)


def spec(space=VMEM):
    return pl.BlockSpec(memory_space=space)


def store_rotary(ref, rotary_t):
    for i in range(DL // TOK):
        ref[TOK:PACK, i * TOK : (i + 1) * TOK] = rotary_t[16 * i : 16 * (i + 1), :].astype(ref.dtype)


def load_rotary(ref):
    parts = [ref[TOK:PACK, i * TOK : (i + 1) * TOK] for i in range(DL // TOK)]
    return jnp.concatenate(parts, axis=0)


def pack_kernel(lat_ref, rot_t_ref, out_ref, sems):
    copies = [pltpu.make_async_copy(lat_ref, out_ref.at[pl.ds(0, TOK), :], sems.at[0])]
    for i in range(DL // TOK):
        place = out_ref.at[pl.ds(TOK, PACK - TOK), pl.ds(i * TOK, TOK)]
        copies.append(
            pltpu.make_async_copy(rot_t_ref.at[pl.ds(16 * i, 16), :], place, sems.at[1 + i])
        )
    for copy in copies:
        copy.start()
    for copy in copies:
        copy.wait()


def pair_kernel(first_ref, second_ref, order_ref, out_ref):
    del order_ref
    out_ref[0:PACK, :] = first_ref[...]
    out_ref[PACK:, :] = second_ref[...]


def head_half(shape, head):
    lane = lax.broadcasted_iota(jnp.int32, shape, 1)
    return (lane >= DR) == (head % 2 == 1)


def rows_kernel(
    lens_ref, shard_ref, q_ref, do_ref, qr_ref, qv_ref, dov_ref, qx_ref, low_ref, qx32_ref, sems
):
    q_copy = pltpu.make_async_copy(q_ref, qv_ref, sems.at[0])
    do_copy = pltpu.make_async_copy(do_ref, dov_ref, sems.at[1])
    q_copy.start()
    do_copy.start()
    for head in range(HEADS):
        pair = qr_ref[:, (head // 2) * 2 * DR : (head // 2 + 1) * 2 * DR].astype(F32)
        qx32_ref[pl.ds(head, TOK, stride=HEADS), :] = jnp.where(
            head_half((TOK, 2 * DR), head), pair, 0.0
        )
    qx_ref[...] = qx32_ref[...].astype(BF16)
    high = lax.broadcasted_iota(jnp.int32, (1, ROWS), 1) // HEADS + FAR
    low = jnp.zeros((1, ROWS), jnp.int32)
    start = (SPAN - shard_ref[0]) * TOK
    for doc in range(lens_ref.shape[0]):
        low = jnp.where(high >= start, start, low)
        start = start + lens_ref[doc]
    low_ref[...] = low
    q_copy.wait()
    do_copy.wait()


def load_keys(ref, slot, keys_ref, rot2_ref):
    rows = slice(slot * TOK, (slot + 1) * TOK)
    keys_ref[rows, :] = ref[0:TOK, :]
    rot_t = load_rotary(ref).astype(F32)
    rot2_ref[rows, :] = jnp.transpose(jnp.concatenate([rot_t, rot_t], axis=0)).astype(BF16)


def near_kernel(
    q_ref, qx_ref, do_ref, own_ref, k2_ref, raw_ref, prob_grad_ref, keys_ref, rot2_ref
):
    load_keys(k2_ref, 0, keys_ref, rot2_ref)
    load_keys(own_ref, 1, keys_ref, rot2_ref)
    raw_ref[...] = dot(keys_ref[...], q_ref[...], NT) + dot(rot2_ref[...], qx_ref[...], NT)
    prob_grad_ref[...] = dot(keys_ref[...], do_ref[...], NT)


def scores_kernel(
    low_ref, q_ref, qx_ref, do_ref, k13_ref, raw_ref, prob_grad_ref, near_ref, near2_ref,
    f13_ref, dst_ref, pt_ref, keys_ref, rot2_ref,
):
    k1_ref = k13_ref.at[pl.ds(0, PACK), :]
    k3_ref = k13_ref.at[pl.ds(PACK, PACK), :]
    load_keys(k3_ref, 0, keys_ref, rot2_ref)
    load_keys(k1_ref, 1, keys_ref, rot2_ref)
    keys_ref[HALF:, :] = near_ref[...]
    rot2_ref[HALF:, :] = near2_ref[...]
    low = low_ref[...]
    high = lax.broadcasted_iota(jnp.int32, (1, ROWS), 1) // HEADS + FAR
    key = lax.broadcasted_iota(jnp.int32, (TOK, CHUNK), 0)
    far = slice(0, HALF)
    for c in range(ROWS // CHUNK):
        cols = slice(c * CHUNK, (c + 1) * CHUNK)
        raw_far = dot(keys_ref[far, :], q_ref[cols, :], NT) + dot(rot2_ref[far, :], qx_ref[cols, :], NT)
        lower = low[:, cols]
        masked = jnp.concatenate(
            [
                jnp.where(key >= lower, raw_far[0:TOK], NEGATIVE),
                jnp.where(key >= lower - 2 * TOK, raw_far[TOK:], NEGATIVE),
                jnp.where(key >= lower - TOK, raw_ref[0:TOK, cols], NEGATIVE),
                jnp.where(
                    (key >= lower - FAR) & (key <= high[:, cols] - FAR), raw_ref[TOK:, cols], NEGATIVE
                ),
            ],
            axis=0,
        )
        peak = jnp.max(masked, axis=0, keepdims=True)
        terms = jnp.exp2((masked - peak) * (SCALE * LOG2_E))
        probs = terms * (1.0 / jnp.sum(terms, axis=0, keepdims=True))
        low_probs = probs.astype(BF16)
        pt_ref[:, cols] = low_probs
        prob_grad = jnp.concatenate(
            [dot(keys_ref[far, :], do_ref[cols, :], NT), prob_grad_ref[:, cols]], axis=0
        )
        delta = jnp.sum(low_probs.astype(F32) * prob_grad, axis=0, keepdims=True)
        dst_ref[:, cols] = (probs * (prob_grad - delta)).astype(BF16)

    grad = SCALE * dot(dst_ref[far, :], q_ref[...], NN) + dot(pt_ref[far, :], do_ref[...], NN)
    rot = SCALE * dot(dst_ref[far, :], qx_ref[...], NN)
    store_tile(f13_ref.at[pl.ds(PACK, PACK), :], grad[0:TOK, :], rot[0:TOK, :])
    store_tile(f13_ref.at[pl.ds(0, PACK), :], grad[TOK:, :], rot[TOK:, :])


def fold_rotary(rot):
    rot_t = jnp.transpose(rot)
    return rot_t[0:DR, :] + rot_t[DR:, :]


def store_tile(ref, grad, rot):
    ref[0:TOK, :] = grad.astype(ref.dtype)
    store_rotary(ref, fold_rotary(rot))


def near_grads_kernel(q_ref, qx_ref, do_ref, dst_ref, pt_ref, f2_ref, g0_ref):
    near = slice(HALF, KEYS)
    grad = SCALE * dot(dst_ref[near, :], q_ref[...], NN) + dot(pt_ref[near, :], do_ref[...], NN)
    rot = SCALE * dot(dst_ref[near, :], qx_ref[...], NN)
    store_tile(f2_ref, grad[0:TOK, :], rot[0:TOK, :])
    store_tile(g0_ref, grad[TOK:, :], rot[TOK:, :])


def queries_kernel(dst_ref, keys_ref, rot2_ref, dq_ref, dqr_ref, x_ref):
    for c in range(ROWS // CHUNK):
        cols = slice(c * CHUNK, (c + 1) * CHUNK)
        ds = jnp.transpose(dst_ref[:, cols])
        dq_ref[cols, :] = (SCALE * dot(ds, keys_ref[...], NN)).astype(BF16)
        x_ref[cols, :] = SCALE * dot(ds, rot2_ref[...], NN)
    for pair in range(HEADS // 2):
        even = x_ref[pl.ds(2 * pair, TOK, stride=HEADS), :]
        odd = x_ref[pl.ds(2 * pair + 1, TOK, stride=HEADS), :]
        dqr_ref[:, pair * 2 * DR : (pair + 1) * 2 * DR] = jnp.where(
            head_half((TOK, 2 * DR), 0), even, odd
        ).astype(BF16)


def relay_kernel(f2_ref, r13_ref, out_ref):
    out_ref[...] = (f2_ref[...] + r13_ref[PACK:, :].astype(F32)).astype(BF16)


def total_kernel(g0_ref, r13_ref, r2_ref, out_ref):
    total = g0_ref[...] + r13_ref[0:PACK, :].astype(F32) + r2_ref[...].astype(F32)
    out_ref[:, 0:DL] = total[0:TOK, :].astype(BF16)
    parts = [total[TOK:, i * TOK : (i + 1) * TOK] for i in range(DL // TOK)]
    rot = jnp.transpose(jnp.concatenate(parts + parts, axis=0))
    out_ref[:, DL:] = rot[:, 0:DR].astype(BF16)


def sum_kernel(blocks_ref, lat_ref, rot_ref):
    total = jnp.sum(blocks_ref[...].astype(F32), axis=0)
    lat_ref[...] = total[:, 0:DL].astype(BF16)
    rot_ref[...] = total[:, DL:].astype(BF16)


def shape(dims, dtype=BF16):
    return jax.ShapeDtypeStruct(dims, dtype)


def call(kernel, outs, spaces, scratch=(), flops=0, moved=0, name=None, limit=24):
    return pl.pallas_call(
        kernel,
        out_shape=outs,
        in_specs=[spec(s) for s in spaces],
        out_specs=jax.tree.map(lambda _: spec(), outs),
        scratch_shapes=scratch,
        compiler_params=pltpu.CompilerParams(vmem_limit_bytes=limit << 20),
        cost_estimate=pl.CostEstimate(flops=flops, bytes_accessed=moved, transcendentals=0),
        name=name,
    )


def pack(latents, rotary_t):
    return call(
        pack_kernel, shape((PACK, DL)), [HBM] * 2,
        scratch=[pltpu.SemaphoreType.DMA((1 + DL // TOK,))], moved=300000, name="pack",
    )(latents, rotary_t)


def pair_up(first, second, order):
    return call(pair_kernel, shape((2 * PACK, DL)), [VMEM] * 3, moved=600000, name="pair")(
        first, second, order
    )


def row_setup(lens, shard, q, do, qr):
    outs = (shape((ROWS, DL)), shape((ROWS, DL)), shape((ROWS, 2 * DR)), shape((1, ROWS), jnp.int32))
    return call(
        rows_kernel, outs, [SMEM, SMEM, HBM, HBM, VMEM],
        scratch=[pltpu.VMEM((ROWS, 2 * DR), F32), pltpu.SemaphoreType.DMA((2,))],
        moved=4 << 20, name="row_setup",
    )(lens, shard, q, do, qr)


def near_scores(q, qx, do, own, k2):
    outs = (
        shape((HALF, ROWS), F32), shape((HALF, ROWS), F32), shape((HALF, DL)), shape((HALF, 2 * DR)),
    )
    return call(
        near_kernel, outs, [VMEM] * 5, flops=2 * ROWS * KEYS * DL, moved=4 << 20, name="near_scores"
    )(q, qx, do, own, k2)


def scores(low, q, qx, do, k13, raw, prob_grad, near, near2):
    outs = (
        shape((2 * PACK, DL)), shape((KEYS, ROWS)), shape((KEYS, ROWS)),
        shape((KEYS, DL)), shape((KEYS, 2 * DR)),
    )
    return call(
        scores_kernel, outs, [VMEM] * 9,
        flops=2 * ROWS * KEYS * DL * 2, moved=6 << 20, name="scores",
    )(low, q, qx, do, k13, raw, prob_grad, near, near2)


def near_grads(q, qx, do, dst, pt):
    tile = shape((PACK, DL), F32)
    return call(
        near_grads_kernel, (tile, tile), [VMEM] * 5,
        flops=2 * ROWS * KEYS * DL, moved=4 << 20, name="near_grads",
    )(q, qx, do, dst, pt)


def queries(dst, keys, rot2):
    outs = (shape((ROWS, DL)), shape((TOK, HEADS * DR)))
    return call(
        queries_kernel, outs, [VMEM] * 3, scratch=[pltpu.VMEM((ROWS, 2 * DR), F32)],
        flops=2 * ROWS * KEYS * DL, moved=4 << 20, name="queries",
    )(dst, keys, rot2)


def relay(f2, r13):
    return call(relay_kernel, shape((PACK, DL)), [VMEM] * 2, moved=600000, name="relay")(f2, r13)


def total(g0, r13, r2):
    return call(total_kernel, shape((TOK, DL + DR)), [VMEM] * 3, moved=1 << 20, name="total")(
        g0, r13, r2
    )


def head_sum(blocks):
    rows = blocks.shape[1]
    return call(
        sum_kernel, (shape((rows, DL)), shape((rows, DR))), [VMEM], moved=200000, name="head_sum"
    )(blocks)


def shifted(block, axis, distance):
    devices = range(lax.axis_size(axis))
    route = [(i - distance, i) for i in devices if i - distance in devices]
    return lax.ppermute(block, axis, route)


def body(query_latent, query_rotary, latents, key_rotary, out_grad, doc_lengths):
    head_devices = lax.axis_size("head")
    shard = jnp.reshape(lax.axis_index("tok"), (1,)).astype(jnp.int32)
    q = query_latent.reshape(ROWS, DL)
    do = out_grad.reshape(ROWS, DL)
    own = pack(latents, key_rotary.T)
    k2 = shifted(own, "tok", 2)
    q, do, qx, low = row_setup(doc_lengths, shard, q, do, query_rotary)
    k13 = shifted(pair_up(own, k2, low), "tok", 1)
    raw, prob_grad, near, near2 = near_scores(q, qx, do, own, k2)
    f13, dst, pt, keys, rot2 = scores(low, q, qx, do, k13, raw, prob_grad, near, near2)
    r13 = shifted(f13, "tok", -1)
    f2, g0 = near_grads(q, qx, do, dst, pt)
    r2 = shifted(relay(f2, r13), "tok", -2)
    dq, dqr = queries(dst, keys, rot2)
    blocks = total(g0, r13, r2).reshape(head_devices, TOK // head_devices, DL + DR)
    blocks = lax.all_to_all(blocks, "head", split_axis=0, concat_axis=0, tiled=True)
    grad_latents, grad_key_rotary = head_sum(blocks)
    return dq.reshape(TOK, HEADS, DL), dqr, grad_latents, grad_key_rotary


def solution(mesh):
    in_specs = (
        P("tok", "head", None),
        P("tok", "head"),
        P("tok", None),
        P("tok", None),
        P("tok", "head", None),
        P(),
    )
    out_specs = (
        P("tok", "head", None),
        P("tok", "head"),
        P(("tok", "head"), None),
        P(("tok", "head"), None),
    )
    return jax.shard_map(body, mesh=mesh, in_specs=in_specs, out_specs=out_specs, check_vma=False)
```

time: 83.2 us -> 74.9 us (0.900); the launches traced: 81.8 us -> 74.4 us
  waiting for transfers between devices: 18 us -> 29 us
  matrix products: 10.6 us -> 0 us
  Pallas kernels: 0 us -> 9.25 us
  local copies, waits for them, and re-layouts: 10.9 us -> 4.71 us
  starting transfers between devices: 36.4 us -> 30.6 us
  other arithmetic: 5.02 us -> 0 us
    ppermute x6 -> x4, waiting for transfers between devices: 7.59 us -> 17 us  [shifted(): return lax.ppermute(block, axis, route)]
    pallas_call x0 -> x10, Pallas kernels: none -> 9.25 us  [the longest x1 2.87 us: scores(): call(scores_kernel, outs, [VMEM] * 9, flops=2 * ROWS * KEYS * DL * 2, mov...]
    dot_general x7 -> x0, matrix products: 7.62 us -> none  [the longest x1 2.88 us: body(): jnp.einsum('qhd,kd->hqk', out_grad, key_latent, preferred_element_type=jn...]
    ppermute x6 -> x4, starting transfers between devices: 17.8 us -> 12.1 us  [shifted(): return lax.ppermute(block, axis, route)]
    unnamed x16 -> x12, local copies, waits for them, and re-layouts: 8.1 us -> 4.71 us
    sub x1 -> x0, matrix products: 2.96 us -> none  [body(): exp_terms = jnp.where(visible[None], jnp.exp(masked - row_max), 0.0)]
    convert_element_type x2 -> x0, other arithmetic: 1.97 us -> none  [the longest x1 1.89 us: body(): score_grad = (attn_probs * (prob_grad - row_delta)).astype(jnp.bfloat16)]
    concatenate x3 -> x0, other arithmetic: 1.84 us -> none  [the longest x1 0.93 us: body(): own_keys = jnp.concatenate([latents, key_rotary], axis=1)]
  transfers between devices with their start and end apart: 7 -> 5, of which waited for: 4 -> 5; matrix products, arithmetic and copies ran while one was open for 12% -> 0% of each run, Pallas kernels for 0% -> 6%
where the time goes in v2:
time: 74.9 us; the launch traced here: 74.4 us
  starting transfers between devices  30.6 us (41%)
  waiting for transfers between devices  29 us (39%)
  Pallas kernels  9.25 us (12%)
  local copies, waits for them, and re-layouts  4.71 us (6%)
  between operations  0.75 us (1%)
    all_to_all x1, starting transfers between devices, body(): lax.all_to_all(blocks, 'head', split_axis=0, concat_axis=0, tiled=True)  18.6 us
    ppermute x4, waiting for transfers between devices, shifted(): return lax.ppermute(block, axis, route)  17 us
    ppermute x4, starting transfers between devices, shifted(): return lax.ppermute(block, axis, route)  12.1 us
    all_to_all x1, waiting for transfers between devices, body(): lax.all_to_all(blocks, 'head', split_axis=0, concat_axis=0, tiled=True)  12 us
    unnamed x12, local copies, waits for them, and re-layouts  4.71 us
    pallas_call x1, Pallas kernels, scores(): call(scores_kernel, outs, [VMEM] * 9, flops=2 * ROWS * KEYS * DL * 2, mov...  2.87 us
    pallas_call x1, Pallas kernels, queries(): call(queries_kernel, outs, [VMEM] * 3, scratch=[pltpu.VMEM((ROWS, 2 * DR)...  1.96 us
  transfers between devices with their start and end apart: 5, of which 5 were waited for; matrix products, arithmetic and copies ran while one was open for 0% of the time, Pallas kernels for 6%

profile of v2, /device:TPU:57, one launch (start us, length us, event | category | flops | bytes accessed | tf_op | source)
XLA Modules:
  0.0 74.4 jit_solution(11614582706075581039)
XLA Ops:
  0.6 0.0 copy-start.3
  0.6 0.9 %copy-done.3 = bf16[128,512]{1,0:T(8,128)(2,1)S(1)} copy-done((bf16[128,512]{1,0:T(8,128)(2,1)S(1)}, bf16[128,512]{1,0:T(8,128)(2,1)}, u32[]{:S(2)}) %copy-start.3) | copy-done | bytes 131096
  1.5 0.0 copy-start.4
  1.5 0.7 copy-done.4
  2.3 0.0 copy-start.2
  2.3 0.2 pack.1.first_ref.own_ref
  2.5 2.3 %collective-permute-start = (bf16[144,512]{1,0:T(8,128)(2,1)S(1)}, bf16[144,512]{1,0:T(8,128)(2,1)S(1)}, u32[]{:S(2)}, u32[]{:S(2)}) collective-permute-start(bf16[144,512]{1,0:T(8,128)(2,1)S(1)} %pack.1.first_ref.own_ref), channel_id=1, source_target_pairs={{0,32},{16,48},{32,64},{48,80},{64,96},{80,112},{96,128},{112,144}... | collective-permute-start | bytes 442376 | tf_op jit(solution)/shard_map/ppermute | solution.py:309
  4.8 0.0 copy-start.5
  4.8 0.0 copy-done.2
  4.8 0.6 copy-done.5
  5.5 0.0 copy-start
  5.5 1.2 %copy-done = bf16[128,8,512]{2,1,0:T(8,128)(2,1)S(1)} copy-done((bf16[128,8,512]{2,1,0:T(8,128)(2,1)S(1)}, bf16[128,8,512]{2,1,0:T(8,128)(2,1)}, u32[]{:S(2)}) %copy-start) | copy-done | bytes 1048600
  6.7 0.0 copy-start.1
  6.7 1.2 %copy-done.1 = bf16[128,8,512]{2,1,0:T(8,128)(2,1)S(1)} copy-done((bf16[128,8,512]{2,1,0:T(8,128)(2,1)S(1)}, bf16[128,8,512]{2,1,0:T(8,128)(2,1)}, u32[]{:S(2)}) %copy-start.1) | copy-done | bytes 1048600
  7.9 0.9 %row_setup.1 = (bf16[1024,512]{1,0:T(8,128)(2,1)S(1)}, bf16[1024,512]{1,0:T(8,128)(2,1)S(1)}, bf16[1024,128]{1,0:T(8,128)(2,1)S(1)}, s32[1,1024]{1,0:T(1,128)S(1)}) custom-call(s32[33]{0:T(128)S(1)} %copy-done.5, s32[1]{0:T(128)} %bitcast.shard_ref, bf16[1024,512]{1,0:T(8,128)(2,1)S(1)} %bitcast.6, bf16[1024,512]{1,0:T(8,128)(2,1)S(1)} %bitcast.7, ...), custom_call_target="tpu_custom_call" | custom-call | bytes 4194304 | tf_op jit(solution)/shard_map/row_setup/pallas_call | solution.py:246
  8.9 0.2 collective-permute-done.second_ref.k2_ref
  9.1 5.8 %collective-permute-start.1 = (bf16[288,512]{1,0:T(8,128)(2,1)S(1)}, bf16[288,512]{1,0:T(8,128)(2,1)S(1)}, u32[]{:S(2)}, u32[]{:S(2)}) collective-permute-start(bf16[288,512]{1,0:T(8,128)(2,1)S(1)} %pair.1), channel_id=1, source_target_pairs={{0,16},{16,32},{32,48},{48,64},{64,80},{80,96},{96,112},{112,128},... | collective-permute-start | bytes 884744 | tf_op jit(solution)/shard_map/ppermute | solution.py:309
  15.0 0.9 %near_scores.1 = (f32[256,1024]{1,0:T(8,128)S(1)}, f32[256,1024]{1,0:T(8,128)S(1)}, bf16[256,512]{1,0:T(8,128)(2,1)S(1)}, bf16[256,128]{1,0:T(8,128)(2,1)S(1)}) custom-call(bf16[1024,512]{1,0:T(8,128)(2,1)S(1)} %get-tuple-element.24.q_ref, bf16[1024,128]{1,0:T(8,128)(2,1)S(1)} %get-tuple-element.25.qx_ref, bf16[1024,512]{1,0:T(8,128)(2,1)S(1)} %get-tuple-element.26.do_ref, ...), custom_call_target="tpu_custom_call" | custom-call | flops 536870912 | bytes 4194304 | tf_op jit(solution)/shard_map/near_scores/pallas_call | solution.py:257
  15.9 2.7 %collective-permute-done.1.k13_ref = bf16[288,512]{1,0:T(8,128)(2,1)S(1)} collective-permute-done((bf16[288,512]{1,0:T(8,128)(2,1)S(1)}, bf16[288,512]{1,0:T(8,128)(2,1)S(1)}, u32[]{:S(2)}, u32[]{:S(2)}) %collective-permute-start.1) | collective-permute-done | bytes 294944 | tf_op jit(solution)/shard_map/ppermute | solution.py:309
  18.6 2.9 %scores.1 = (bf16[288,512]{1,0:T(8,128)(2,1)S(1)}, bf16[512,1024]{1,0:T(8,128)(2,1)S(1)}, bf16[512,1024]{1,0:T(8,128)(2,1)S(1)}, bf16[512,512]{1,0:T(8,128)(2,1)S(1)}, bf16[512,128]{1,0:T(8,128)(2,1)S(1)}) custom-call(s32[1,1024]{1,0:T(1,128)S(1)} %get-tuple-element.23.order_ref.low_ref, bf16[1024,512]{1,0:T(8,128)(2,1)S(1)} %get-tuple-element.24.q_ref, ...), custom_call_target="tpu_custom_call" | custom-call | flops 1073741824 | bytes 6291456 | tf_op jit(solution)/shard_map/scores/pallas_call | solution.py:267
  21.5 2.0 %collective-permute-start.2 = (bf16[288,512]{1,0:T(8,128)(2,1)S(1)}, bf16[288,512]{1,0:T(8,128)(2,1)S(1)}, u32[]{:S(2)}, u32[]{:S(2)}) collective-permute-start(bf16[288,512]{1,0:T(8,128)(2,1)S(1)} %get-tuple-element.38), channel_id=1, source_target_pairs={{16,0},{32,16},{48,32},{64,48},{80,64},{96,80},{112,96},{128,112},... | collective-permute-start | bytes 884744 | tf_op jit(solution)/shard_map/ppermute | solution.py:309
  23.5 0.9 %near_grads.1 = (f32[144,512]{1,0:T(8,128)S(1)}, f32[144,512]{1,0:T(8,128)S(1)}) custom-call(bf16[1024,512]{1,0:T(8,128)(2,1)S(1)} %get-tuple-element.24.q_ref, bf16[1024,128]{1,0:T(8,128)(2,1)S(1)} %get-tuple-element.25.qx_ref, bf16[1024,512]{1,0:T(8,128)(2,1)S(1)} %get-tuple-element.26.do_ref, bf16[512,1024]{1,0:T(8,128)(2,1)S(1)} %get-tuple-element.31.dst_ref, ...), custom_call_target="tpu_custom_call" | custom-call | flops 536870912 | bytes 4194304 | tf_op jit(solution)/shard_map/near_grads/pallas_call | solution.py:275
  24.4 8.0 %collective-permute-done.2.r13_ref = bf16[288,512]{1,0:T(8,128)(2,1)S(1)} collective-permute-done((bf16[288,512]{1,0:T(8,128)(2,1)S(1)}, bf16[288,512]{1,0:T(8,128)(2,1)S(1)}, u32[]{:S(2)}, u32[]{:S(2)}) %collective-permute-start.2) | collective-permute-done | bytes 294944 | tf_op jit(solution)/shard_map/ppermute | solution.py:309
  32.4 1.9 %collective-permute-start.3 = (bf16[144,512]{1,0:T(8,128)(2,1)S(1)}, bf16[144,512]{1,0:T(8,128)(2,1)S(1)}, u32[]{:S(2)}, u32[]{:S(2)}) collective-permute-start(bf16[144,512]{1,0:T(8,128)(2,1)S(1)} %relay.1), channel_id=1, source_target_pairs={{32,0},{48,16},{64,32},{80,48},{96,64},{112,80},{128,96},{144,112}... | collective-permute-start | bytes 442376 | tf_op jit(solution)/shard_map/ppermute | solution.py:309
  34.4 6.1 %collective-permute-done.3.r2_ref = bf16[144,512]{1,0:T(8,128)(2,1)S(1)} collective-permute-done((bf16[144,512]{1,0:T(8,128)(2,1)S(1)}, bf16[144,512]{1,0:T(8,128)(2,1)S(1)}, u32[]{:S(2)}, u32[]{:S(2)}) %collective-permute-start.3) | collective-permute-done | bytes 147488 | tf_op jit(solution)/shard_map/ppermute | solution.py:309
  40.4 0.8 %total.1 = bf16[128,576]{1,0:T(8,128)(2,1)} custom-call(f32[144,512]{1,0:T(8,128)S(1)} %get-tuple-element.37.g0_ref, bf16[288,512]{1,0:T(8,128)(2,1)S(1)} %collective-permute-done.2.r13_ref, bf16[144,512]{1,0:T(8,128)(2,1)S(1)} %collective-permute-done.3.r2_ref), custom_call_target="tpu_custom_call" | custom-call | bytes 1048576 | tf_op jit(solution)/shard_map/total/pallas_call | solution.py:294
  41.2 18.6 %all-to-all-start = ((bf16[16,8,576]{2,1,0:T(8,128)(2,1)}), bf16[16,8,576]{2,1,0:T(8,128)(2,1)S(1)}, u32[]{:S(2)}, u32[]{:S(2)}) async-start(bf16[16,8,576]{2,1,0:T(8,128)(2,1)} %bitcast.5), calls=%async_computation | async-start | bytes 327680 | tf_op jit(solution)/shard_map/all_to_all | solution.py:328
  59.8 2.0 %queries.1 = (bf16[1024,512]{1,0:T(8,128)(2,1)}, bf16[128,512]{1,0:T(8,128)(2,1)}) custom-call(bf16[512,1024]{1,0:T(8,128)(2,1)S(1)} %get-tuple-element.31.dst_ref, bf16[512,512]{1,0:T(8,128)(2,1)S(1)} %get-tuple-element.32.keys_ref, bf16[512,128]{1,0:T(8,128)(2,1)S(1)} %get-tuple-element.33.rot2_ref), custom_call_target="tpu_custom_call" | custom-call | flops 536870912 | bytes 4194304 | tf_op jit(solution)/shard_map/queries/pallas_call | solution.py:283
  61.8 12.0 %all-to-all-done.blocks_ref = bf16[16,8,576]{2,1,0:T(8,128)(2,1)S(1)} async-done(((bf16[16,8,576]{2,1,0:T(8,128)(2,1)}), bf16[16,8,576]{2,1,0:T(8,128)(2,1)S(1)}, u32[]{:S(2)}, u32[]{:S(2)}) %all-to-all-start) | async-done | bytes 147488 | tf_op jit(solution)/shard_map/all_to_all | solution.py:328
  73.8 0.6 head_sum.1
  (2 shorter events, 0.0 us)
Async XLA Ops:
  0.6 0.9 %copy-start.3 = (bf16[128,512]{1,0:T(8,128)(2,1)S(1)}, bf16[128,512]{1,0:T(8,128)(2,1)}, u32[]{:S(2)}) copy-start(bf16[128,512]{1,0:T(8,128)(2,1)} %lat_ref.1) | copy-start | bytes 393220
  1.5 0.7 copy-start.4
  2.3 2.6 %copy-start.2 = (bf16[128,512]{1,0:T(8,128)(2,1)S(1)}, bf16[128,512]{1,0:T(8,128)(2,1)}, u32[]{:S(2)}) copy-start(bf16[128,512]{1,0:T(8,128)(2,1)} %qr_ref.1) | copy-start | bytes 393220
  2.5 6.6 %collective-permute-start = (bf16[144,512]{1,0:T(8,128)(2,1)S(1)}, bf16[144,512]{1,0:T(8,128)(2,1)S(1)}, u32[]{:S(2)}, u32[]{:S(2)}) collective-permute-start(bf16[144,512]{1,0:T(8,128)(2,1)S(1)} %pack.1.first_ref.own_ref), channel_id=1, source_target_pairs={{0,32},{16,48},{32,64},{48,80},{64,96},{80,112},{96,128},{112,144}... | collective-permute-start | bytes 442376 | tf_op jit(solution)/shard_map/ppermute | solution.py:309
  4.8 0.7 copy-start.5
  5.5 1.2 %copy-start = (bf16[128,8,512]{2,1,0:T(8,128)(2,1)S(1)}, bf16[128,8,512]{2,1,0:T(8,128)(2,1)}, u32[]{:S(2)}) copy-start(bf16[128,8,512]{2,1,0:T(8,128)(2,1)} %param.6) | copy-start | bytes 3145732
  6.7 1.2 %copy-start.1 = (bf16[128,8,512]{2,1,0:T(8,128)(2,1)S(1)}, bf16[128,8,512]{2,1,0:T(8,128)(2,1)}, u32[]{:S(2)}) copy-start(bf16[128,8,512]{2,1,0:T(8,128)(2,1)} %param.10) | copy-start | bytes 3145732
  9.1 9.5 %collective-permute-start.1 = (bf16[288,512]{1,0:T(8,128)(2,1)S(1)}, bf16[288,512]{1,0:T(8,128)(2,1)S(1)}, u32[]{:S(2)}, u32[]{:S(2)}) collective-permute-start(bf16[288,512]{1,0:T(8,128)(2,1)S(1)} %pair.1), channel_id=1, source_target_pairs={{0,16},{16,32},{32,48},{48,64},{64,80},{80,96},{96,112},{112,128},... | collective-permute-start | bytes 884744 | tf_op jit(solution)/shard_map/ppermute | solution.py:309
  21.5 10.9 %collective-permute-start.2 = (bf16[288,512]{1,0:T(8,128)(2,1)S(1)}, bf16[288,512]{1,0:T(8,128)(2,1)S(1)}, u32[]{:S(2)}, u32[]{:S(2)}) collective-permute-start(bf16[288,512]{1,0:T(8,128)(2,1)S(1)} %get-tuple-element.38), channel_id=1, source_target_pairs={{16,0},{32,16},{48,32},{64,48},{80,64},{96,80},{112,96},{128,112},... | collective-permute-start | bytes 884744 | tf_op jit(solution)/shard_map/ppermute | solution.py:309
  32.4 8.0 %collective-permute-start.3 = (bf16[144,512]{1,0:T(8,128)(2,1)S(1)}, bf16[144,512]{1,0:T(8,128)(2,1)S(1)}, u32[]{:S(2)}, u32[]{:S(2)}) collective-permute-start(bf16[144,512]{1,0:T(8,128)(2,1)S(1)} %relay.1), channel_id=1, source_target_pairs={{32,0},{48,16},{64,32},{80,48},{96,64},{112,80},{128,96},{144,112}... | collective-permute-start | bytes 442376 | tf_op jit(solution)/shard_map/ppermute | solution.py:309
  41.2 32.6 %all-to-all-start = ((bf16[16,8,576]{2,1,0:T(8,128)(2,1)}), bf16[16,8,576]{2,1,0:T(8,128)(2,1)S(1)}, u32[]{:S(2)}, u32[]{:S(2)}) async-start(bf16[16,8,576]{2,1,0:T(8,128)(2,1)} %bitcast.5), calls=%async_computation | async-start | bytes 327680 | tf_op jit(solution)/shard_map/all_to_all | solution.py:328

commit v3 on v2

--- a/solution.py
+++ b/solution.py
@@ -197,7 +197,8 @@
     out_ref[...] = (f2_ref[...] + r13_ref[PACK:, :].astype(F32)).astype(BF16)
 
 
-def total_kernel(g0_ref, r13_ref, r2_ref, out_ref):
+def total_kernel(g0_ref, r13_ref, r2_ref, order_ref, out_ref):
+    del order_ref
     total = g0_ref[...] + r13_ref[0:PACK, :].astype(F32) + r2_ref[...].astype(F32)
     out_ref[:, 0:DL] = total[0:TOK, :].astype(BF16)
     parts = [total[TOK:, i * TOK : (i + 1) * TOK] for i in range(DL // TOK)]
@@ -228,6 +229,10 @@
     )
 
 
+def in_hbm(x):
+    return pltpu.with_memory_space_constraint(x, pltpu.HBM)
+
+
 def pack(latents, rotary_t):
     return call(
         pack_kernel, shape((PACK, DL)), [HBM] * 2,
@@ -290,10 +295,10 @@
     return call(relay_kernel, shape((PACK, DL)), [VMEM] * 2, moved=600000, name="relay")(f2, r13)
 
 
-def total(g0, r13, r2):
-    return call(total_kernel, shape((TOK, DL + DR)), [VMEM] * 3, moved=1 << 20, name="total")(
-        g0, r13, r2
-    )
+def total(g0, r13, r2, order):
+    return call(
+        total_kernel, shape((TOK, DL + DR)), [VMEM] * 3 + [HBM], moved=1 << 20, name="total"
+    )(g0, r13, r2, order)
 
 
 def head_sum(blocks):
@@ -314,9 +319,9 @@
     shard = jnp.reshape(lax.axis_index("tok"), (1,)).astype(jnp.int32)
     q = query_latent.reshape(ROWS, DL)
     do = out_grad.reshape(ROWS, DL)
-    own = pack(latents, key_rotary.T)
+    own = pack(in_hbm(latents), in_hbm(key_rotary.T))
     k2 = shifted(own, "tok", 2)
-    q, do, qx, low = row_setup(doc_lengths, shard, q, do, query_rotary)
+    q, do, qx, low = row_setup(doc_lengths, shard, in_hbm(q), in_hbm(do), query_rotary)
     k13 = shifted(pair_up(own, k2, low), "tok", 1)
     raw, prob_grad, near, near2 = near_scores(q, qx, do, own, k2)
     f13, dst, pt, keys, rot2 = scores(low, q, qx, do, k13, raw, prob_grad, near, near2)
@@ -324,7 +329,7 @@
     f2, g0 = near_grads(q, qx, do, dst, pt)
     r2 = shifted(relay(f2, r13), "tok", -2)
     dq, dqr = queries(dst, keys, rot2)
-    blocks = total(g0, r13, r2).reshape(head_devices, TOK // head_devices, DL + DR)
+    blocks = total(g0, r13, r2, in_hbm(dqr)).reshape(head_devices, TOK // head_devices, DL + DR)
     blocks = lax.all_to_all(blocks, "head", split_axis=0, concat_axis=0, tiled=True)
     grad_latents, grad_key_rotary = head_sum(blocks)
     return dq.reshape(TOK, HEADS, DL), dqr, grad_latents, grad_key_rotary

time: 74.9 us -> 73 us (0.975)
  blocking collectives: 0 us -> 32.4 us
  starting transfers between devices: 30.6 us -> 12.1 us
  waiting for transfers between devices: 29 us -> 16.4 us
  local copies, waits for them, and re-layouts: 4.71 us -> 0.64 us
  Pallas kernels: 9.25 us -> 10.6 us
    all_to_all x0 -> x1, blocking collectives: none -> 32.4 us  [body(): lax.all_to_all(blocks, 'head', split_axis=0, concat_axis=0, tiled=True)]
    all_to_all x1 -> x0, starting transfers between devices: 18.6 us -> none  [body(): lax.all_to_all(blocks, 'head', split_axis=0, concat_axis=0, tiled=True)]
    all_to_all x1 -> x0, waiting for transfers between devices: 12 us -> none  [body(): lax.all_to_all(blocks, 'head', split_axis=0, concat_axis=0, tiled=True)]
    unnamed x12 -> x4, local copies, waits for them, and re-layouts: 4.71 us -> 0.64 us
    pallas_call x1, Pallas kernels: 0.93 us -> 2.1 us  [row_setup(): call(rows_kernel, outs, [SMEM, SMEM, HBM, HBM, VMEM], scratch=[pltpu.VMEM...]
    pallas_call x1, Pallas kernels: 0.2 us -> 0.99 us  [pack(): call(pack_kernel, shape((PACK, DL)), [HBM] * 2, scratch=[pltpu.SemaphoreT...]
  transfers between devices with their start and end apart: 5 -> 4, of which waited for: 5 -> 4; matrix products, arithmetic and copies ran while one was open for 0% -> 0% of each run, Pallas kernels for 6% -> 8%
where the time goes in v3:
time: 73 us; the launch traced here: 72.8 us
  blocking collectives  32.4 us (44%)
  waiting for transfers between devices  16.4 us (22%)
  starting transfers between devices  12.1 us (17%)
  Pallas kernels  10.6 us (15%)
  between operations  0.75 us (1%)
    all_to_all x1, blocking collectives, body(): lax.all_to_all(blocks, 'head', split_axis=0, concat_axis=0, tiled=True)  32.4 us
    ppermute x4, waiting for transfers between devices, shifted(): return lax.ppermute(block, axis, route)  16.4 us
    ppermute x4, starting transfers between devices, shifted(): return lax.ppermute(block, axis, route)  12.1 us
    pallas_call x1, Pallas kernels, scores(): call(scores_kernel, outs, [VMEM] * 9, flops=2 * ROWS * KEYS * DL * 2, mov...  2.89 us
    pallas_call x1, Pallas kernels, row_setup(): call(rows_kernel, outs, [SMEM, SMEM, HBM, HBM, VMEM], scratch=[pltpu.VMEM...  2.1 us
    pallas_call x1, Pallas kernels, queries(): call(queries_kernel, outs, [VMEM] * 3, scratch=[pltpu.VMEM((ROWS, 2 * DR)...  1.98 us
  transfers between devices with their start and end apart: 4, of which 4 were waited for; matrix products, arithmetic and copies ran while one was open for 0% of the time, Pallas kernels for 8%

profile of v3, /device:TPU:57, one launch (start us, length us, event | category | flops | bytes accessed | tf_op | source)
XLA Modules:
  0.0 72.8 jit_solution(11776471048640829279)
XLA Ops:
  0.6 0.0 copy-start
  0.6 1.0 %pack.1.first_ref.own_ref = bf16[144,512]{1,0:T(8,128)(2,1)S(1)} custom-call(bf16[128,512]{1,0:T(8,128)(2,1)} %lat_ref.1, bf16[64,128]{1,0:T(8,128)(2,1)} %bitcast.9), custom_call_target="tpu_custom_call" | custom-call | bytes 300000 | tf_op jit(solution)/shard_map/pack/pallas_call | solution.py:237
  1.6 2.3 %collective-permute-start = (bf16[144,512]{1,0:T(8,128)(2,1)S(1)}, bf16[144,512]{1,0:T(8,128)(2,1)S(1)}, u32[]{:S(2)}, u32[]{:S(2)}) collective-permute-start(bf16[144,512]{1,0:T(8,128)(2,1)S(1)} %pack.1.first_ref.own_ref), channel_id=1, source_target_pairs={{0,32},{16,48},{32,64},{48,80},{64,96},{80,112},{96,128},{112,144}... | collective-permute-start | bytes 442376 | tf_op jit(solution)/shard_map/ppermute | solution.py:314
  4.0 0.0 copy-start.1
  4.0 0.0 copy-done
  4.0 0.6 copy-done.1
  4.6 2.1 %row_setup.1 = (bf16[1024,512]{1,0:T(8,128)(2,1)S(1)}, bf16[1024,512]{1,0:T(8,128)(2,1)S(1)}, bf16[1024,128]{1,0:T(8,128)(2,1)S(1)}, s32[1,1024]{1,0:T(1,128)S(1)}) custom-call(s32[33]{0:T(128)S(1)} %copy-done.1, s32[1]{0:T(128)} %bitcast.shard_ref, bf16[1024,512]{1,0:T(8,128)(2,1)} %bitcast.7, bf16[1024,512]{1,0:T(8,128)(2,1)} %bitcast.8, ...), custom_call_target="tpu_custom_call" | custom-call | bytes 4194304 | tf_op jit(solution)/shard_map/row_setup/pallas_call | solution.py:251
  6.7 1.5 %collective-permute-done.second_ref.k2_ref = bf16[144,512]{1,0:T(8,128)(2,1)S(1)} collective-permute-done((bf16[144,512]{1,0:T(8,128)(2,1)S(1)}, bf16[144,512]{1,0:T(8,128)(2,1)S(1)}, u32[]{:S(2)}, u32[]{:S(2)}) %collective-permute-start) | collective-permute-done | bytes 147488 | tf_op jit(solution)/shard_map/ppermute | solution.py:314
  8.3 5.8 %collective-permute-start.1 = (bf16[288,512]{1,0:T(8,128)(2,1)S(1)}, bf16[288,512]{1,0:T(8,128)(2,1)S(1)}, u32[]{:S(2)}, u32[]{:S(2)}) collective-permute-start(bf16[288,512]{1,0:T(8,128)(2,1)S(1)} %pair.1), channel_id=1, source_target_pairs={{0,16},{16,32},{32,48},{48,64},{64,80},{80,96},{96,112},{112,128},... | collective-permute-start | bytes 884744 | tf_op jit(solution)/shard_map/ppermute | solution.py:314
  14.1 0.9 %near_scores.1 = (f32[256,1024]{1,0:T(8,128)S(1)}, f32[256,1024]{1,0:T(8,128)S(1)}, bf16[256,512]{1,0:T(8,128)(2,1)S(1)}, bf16[256,128]{1,0:T(8,128)(2,1)S(1)}) custom-call(bf16[1024,512]{1,0:T(8,128)(2,1)S(1)} %get-tuple-element.24.q_ref, bf16[1024,128]{1,0:T(8,128)(2,1)S(1)} %get-tuple-element.25.qx_ref, bf16[1024,512]{1,0:T(8,128)(2,1)S(1)} %get-tuple-element.26.do_ref, ...), custom_call_target="tpu_custom_call" | custom-call | flops 536870912 | bytes 4194304 | tf_op jit(solution)/shard_map/near_scores/pallas_call | solution.py:262
  15.1 2.7 %collective-permute-done.1.k13_ref = bf16[288,512]{1,0:T(8,128)(2,1)S(1)} collective-permute-done((bf16[288,512]{1,0:T(8,128)(2,1)S(1)}, bf16[288,512]{1,0:T(8,128)(2,1)S(1)}, u32[]{:S(2)}, u32[]{:S(2)}) %collective-permute-start.1) | collective-permute-done | bytes 294944 | tf_op jit(solution)/shard_map/ppermute | solution.py:314
  17.8 2.9 %scores.1 = (bf16[288,512]{1,0:T(8,128)(2,1)S(1)}, bf16[512,1024]{1,0:T(8,128)(2,1)S(1)}, bf16[512,1024]{1,0:T(8,128)(2,1)S(1)}, bf16[512,512]{1,0:T(8,128)(2,1)S(1)}, bf16[512,128]{1,0:T(8,128)(2,1)S(1)}) custom-call(s32[1,1024]{1,0:T(1,128)S(1)} %get-tuple-element.23.order_ref.low_ref, bf16[1024,512]{1,0:T(8,128)(2,1)S(1)} %get-tuple-element.24.q_ref, ...), custom_call_target="tpu_custom_call" | custom-call | flops 1073741824 | bytes 6291456 | tf_op jit(solution)/shard_map/scores/pallas_call | solution.py:272
  20.7 2.0 %collective-permute-start.2 = (bf16[288,512]{1,0:T(8,128)(2,1)S(1)}, bf16[288,512]{1,0:T(8,128)(2,1)S(1)}, u32[]{:S(2)}, u32[]{:S(2)}) collective-permute-start(bf16[288,512]{1,0:T(8,128)(2,1)S(1)} %get-tuple-element.38), channel_id=1, source_target_pairs={{16,0},{32,16},{48,32},{64,48},{80,64},{96,80},{112,96},{128,112},... | collective-permute-start | bytes 884744 | tf_op jit(solution)/shard_map/ppermute | solution.py:314
  22.7 0.9 %near_grads.1 = (f32[144,512]{1,0:T(8,128)S(1)}, f32[144,512]{1,0:T(8,128)S(1)}) custom-call(bf16[1024,512]{1,0:T(8,128)(2,1)S(1)} %get-tuple-element.24.q_ref, bf16[1024,128]{1,0:T(8,128)(2,1)S(1)} %get-tuple-element.25.qx_ref, bf16[1024,512]{1,0:T(8,128)(2,1)S(1)} %get-tuple-element.26.do_ref, bf16[512,1024]{1,0:T(8,128)(2,1)S(1)} %get-tuple-element.31.dst_ref, ...), custom_call_target="tpu_custom_call" | custom-call | flops 536870912 | bytes 4194304 | tf_op jit(solution)/shard_map/near_grads/pallas_call | solution.py:280
  23.6 8.0 %collective-permute-done.2.r13_ref = bf16[288,512]{1,0:T(8,128)(2,1)S(1)} collective-permute-done((bf16[288,512]{1,0:T(8,128)(2,1)S(1)}, bf16[288,512]{1,0:T(8,128)(2,1)S(1)}, u32[]{:S(2)}, u32[]{:S(2)}) %collective-permute-start.2) | collective-permute-done | bytes 294944 | tf_op jit(solution)/shard_map/ppermute | solution.py:314
  31.6 1.9 %collective-permute-start.3 = (bf16[144,512]{1,0:T(8,128)(2,1)S(1)}, bf16[144,512]{1,0:T(8,128)(2,1)S(1)}, u32[]{:S(2)}, u32[]{:S(2)}) collective-permute-start(bf16[144,512]{1,0:T(8,128)(2,1)S(1)} %relay.1), channel_id=1, source_target_pairs={{32,0},{48,16},{64,32},{80,48},{96,64},{112,80},{128,96},{144,112}... | collective-permute-start | bytes 442376 | tf_op jit(solution)/shard_map/ppermute | solution.py:314
  33.6 2.0 %queries.1 = (bf16[1024,512]{1,0:T(8,128)(2,1)}, bf16[128,512]{1,0:T(8,128)(2,1)}) custom-call(bf16[512,1024]{1,0:T(8,128)(2,1)S(1)} %get-tuple-element.31.dst_ref, bf16[512,512]{1,0:T(8,128)(2,1)S(1)} %get-tuple-element.32.keys_ref, bf16[512,128]{1,0:T(8,128)(2,1)S(1)} %get-tuple-element.33.rot2_ref), custom_call_target="tpu_custom_call" | custom-call | flops 536870912 | bytes 4194304 | tf_op jit(solution)/shard_map/queries/pallas_call | solution.py:288
  35.5 4.1 %collective-permute-done.3.r2_ref = bf16[144,512]{1,0:T(8,128)(2,1)S(1)} collective-permute-done((bf16[144,512]{1,0:T(8,128)(2,1)S(1)}, bf16[144,512]{1,0:T(8,128)(2,1)S(1)}, u32[]{:S(2)}, u32[]{:S(2)}) %collective-permute-start.3) | collective-permute-done | bytes 147488 | tf_op jit(solution)/shard_map/ppermute | solution.py:314
  39.6 0.1 total.1
  39.8 32.4 %all_to_all.5.blocks_ref = bf16[16,8,576]{2,1,0:T(8,128)(2,1)S(1)} all-to-all(bf16[16,8,576]{2,1,0:T(8,128)(2,1)S(1)} %bitcast.6), channel_id=1, replica_groups=mesh['tok'=64,'head'=16] {'head'}, dimensions={0} | all-to-all | bytes 294912 | tf_op jit(solution)/shard_map/all_to_all | solution.py:333
  72.1 0.6 head_sum.1
  (2 shorter events, 0.0 us)
Async XLA Ops:
  0.6 3.4 %copy-start = (bf16[128,512]{1,0:T(8,128)(2,1)S(1)}, bf16[128,512]{1,0:T(8,128)(2,1)}, u32[]{:S(2)}) copy-start(bf16[128,512]{1,0:T(8,128)(2,1)} %qr_ref.1) | copy-start | bytes 393220
  1.6 6.6 %collective-permute-start = (bf16[144,512]{1,0:T(8,128)(2,1)S(1)}, bf16[144,512]{1,0:T(8,128)(2,1)S(1)}, u32[]{:S(2)}, u32[]{:S(2)}) collective-permute-start(bf16[144,512]{1,0:T(8,128)(2,1)S(1)} %pack.1.first_ref.own_ref), channel_id=1, source_target_pairs={{0,32},{16,48},{32,64},{48,80},{64,96},{80,112},{96,128},{112,144}... | collective-permute-start | bytes 442376 | tf_op jit(solution)/shard_map/ppermute | solution.py:314
  4.0 0.7 copy-start.1
  8.3 9.5 %collective-permute-start.1 = (bf16[288,512]{1,0:T(8,128)(2,1)S(1)}, bf16[288,512]{1,0:T(8,128)(2,1)S(1)}, u32[]{:S(2)}, u32[]{:S(2)}) collective-permute-start(bf16[288,512]{1,0:T(8,128)(2,1)S(1)} %pair.1), channel_id=1, source_target_pairs={{0,16},{16,32},{32,48},{48,64},{64,80},{80,96},{96,112},{112,128},... | collective-permute-start | bytes 884744 | tf_op jit(solution)/shard_map/ppermute | solution.py:314
  20.7 10.9 %collective-permute-start.2 = (bf16[288,512]{1,0:T(8,128)(2,1)S(1)}, bf16[288,512]{1,0:T(8,128)(2,1)S(1)}, u32[]{:S(2)}, u32[]{:S(2)}) collective-permute-start(bf16[288,512]{1,0:T(8,128)(2,1)S(1)} %get-tuple-element.38), channel_id=1, source_target_pairs={{16,0},{32,16},{48,32},{64,48},{80,64},{96,80},{112,96},{128,112},... | collective-permute-start | bytes 884744 | tf_op jit(solution)/shard_map/ppermute | solution.py:314
  31.6 8.0 %collective-permute-start.3 = (bf16[144,512]{1,0:T(8,128)(2,1)S(1)}, bf16[144,512]{1,0:T(8,128)(2,1)S(1)}, u32[]{:S(2)}, u32[]{:S(2)}) collective-permute-start(bf16[144,512]{1,0:T(8,128)(2,1)S(1)} %relay.1), channel_id=1, source_target_pairs={{32,0},{48,16},{64,32},{80,48},{96,64},{112,80},{128,96},{144,112}... | collective-permute-start | bytes 442376 | tf_op jit(solution)/shard_map/ppermute | solution.py:314

commit v4 on v3

--- a/solution.py
+++ b/solution.py
@@ -62,12 +62,6 @@
         copy.start()
     for copy in copies:
         copy.wait()
-
-
-def pair_kernel(first_ref, second_ref, order_ref, out_ref):
-    del order_ref
-    out_ref[0:PACK, :] = first_ref[...]
-    out_ref[PACK:, :] = second_ref[...]
 
 
 def head_half(shape, head):
@@ -116,11 +110,9 @@
 
 
 def scores_kernel(
-    low_ref, q_ref, qx_ref, do_ref, k13_ref, raw_ref, prob_grad_ref, near_ref, near2_ref,
-    f13_ref, dst_ref, pt_ref, keys_ref, rot2_ref,
+    low_ref, q_ref, qx_ref, do_ref, k1_ref, k3_ref, raw_ref, prob_grad_ref, near_ref, near2_ref,
+    f3_ref, f2_ref, f1_ref, dst_ref, pt_ref, keys_ref, rot2_ref,
 ):
-    k1_ref = k13_ref.at[pl.ds(0, PACK), :]
-    k3_ref = k13_ref.at[pl.ds(PACK, PACK), :]
     load_keys(k3_ref, 0, keys_ref, rot2_ref)
     load_keys(k1_ref, 1, keys_ref, rot2_ref)
     keys_ref[HALF:, :] = near_ref[...]
@@ -155,10 +147,12 @@
         delta = jnp.sum(low_probs.astype(F32) * prob_grad, axis=0, keepdims=True)
         dst_ref[:, cols] = (probs * (prob_grad - delta)).astype(BF16)
 
-    grad = SCALE * dot(dst_ref[far, :], q_ref[...], NN) + dot(pt_ref[far, :], do_ref[...], NN)
-    rot = SCALE * dot(dst_ref[far, :], qx_ref[...], NN)
-    store_tile(f13_ref.at[pl.ds(PACK, PACK), :], grad[0:TOK, :], rot[0:TOK, :])
-    store_tile(f13_ref.at[pl.ds(0, PACK), :], grad[TOK:, :], rot[TOK:, :])
+    earlier = slice(0, FAR)
+    grad = SCALE * dot(dst_ref[earlier, :], q_ref[...], NN) + dot(pt_ref[earlier, :], do_ref[...], NN)
+    rot = SCALE * dot(dst_ref[earlier, :], qx_ref[...], NN)
+    for slot, ref in enumerate((f3_ref, f1_ref, f2_ref)):
+        rows = slice(slot * TOK, (slot + 1) * TOK)
+        store_tile(ref, grad[rows, :], rot[rows, :])
 
 
 def fold_rotary(rot):
@@ -171,15 +165,12 @@
     store_rotary(ref, fold_rotary(rot))
 
 
-def near_grads_kernel(q_ref, qx_ref, do_ref, dst_ref, pt_ref, f2_ref, g0_ref):
-    near = slice(HALF, KEYS)
-    grad = SCALE * dot(dst_ref[near, :], q_ref[...], NN) + dot(pt_ref[near, :], do_ref[...], NN)
-    rot = SCALE * dot(dst_ref[near, :], qx_ref[...], NN)
-    store_tile(f2_ref, grad[0:TOK, :], rot[0:TOK, :])
-    store_tile(g0_ref, grad[TOK:, :], rot[TOK:, :])
-
-
-def queries_kernel(dst_ref, keys_ref, rot2_ref, dq_ref, dqr_ref, x_ref):
+def queries_kernel(
+    q_ref, qx_ref, do_ref, dst_ref, pt_ref, keys_ref, rot2_ref, dq_ref, dqr_ref, g0_ref, x_ref
+):
+    own = slice(FAR, KEYS)
+    grad = SCALE * dot(dst_ref[own, :], q_ref[...], NN) + dot(pt_ref[own, :], do_ref[...], NN)
+    store_tile(g0_ref, grad, SCALE * dot(dst_ref[own, :], qx_ref[...], NN))
     for c in range(ROWS // CHUNK):
         cols = slice(c * CHUNK, (c + 1) * CHUNK)
         ds = jnp.transpose(dst_ref[:, cols])
@@ -193,13 +184,10 @@
         ).astype(BF16)
 
 
-def relay_kernel(f2_ref, r13_ref, out_ref):
-    out_ref[...] = (f2_ref[...] + r13_ref[PACK:, :].astype(F32)).astype(BF16)
-
-
-def total_kernel(g0_ref, r13_ref, r2_ref, order_ref, out_ref):
-    del order_ref
-    total = g0_ref[...] + r13_ref[0:PACK, :].astype(F32) + r2_ref[...].astype(F32)
+def total_kernel(g0_ref, r1_ref, r2_ref, r3_ref, out_ref):
+    total = g0_ref[...]
+    for ref in (r1_ref, r2_ref, r3_ref):
+        total = total + ref[...].astype(F32)
     out_ref[:, 0:DL] = total[0:TOK, :].astype(BF16)
     parts = [total[TOK:, i * TOK : (i + 1) * TOK] for i in range(DL // TOK)]
     rot = jnp.transpose(jnp.concatenate(parts + parts, axis=0))
@@ -240,12 +228,6 @@
     )(latents, rotary_t)
 
 
-def pair_up(first, second, order):
-    return call(pair_kernel, shape((2 * PACK, DL)), [VMEM] * 3, moved=600000, name="pair")(
-        first, second, order
-    )
-
-
 def row_setup(lens, shard, q, do, qr):
     outs = (shape((ROWS, DL)), shape((ROWS, DL)), shape((ROWS, 2 * DR)), shape((1, ROWS), jnp.int32))
     return call(
@@ -264,41 +246,30 @@
     )(q, qx, do, own, k2)
 
 
-def scores(low, q, qx, do, k13, raw, prob_grad, near, near2):
+def scores(low, q, qx, do, k1, k3, raw, prob_grad, near, near2):
+    tile = shape((PACK, DL))
     outs = (
-        shape((2 * PACK, DL)), shape((KEYS, ROWS)), shape((KEYS, ROWS)),
+        tile, tile, tile, shape((KEYS, ROWS)), shape((KEYS, ROWS)),
         shape((KEYS, DL)), shape((KEYS, 2 * DR)),
     )
     return call(
-        scores_kernel, outs, [VMEM] * 9,
+        scores_kernel, outs, [VMEM] * 10,
         flops=2 * ROWS * KEYS * DL * 2, moved=6 << 20, name="scores",
-    )(low, q, qx, do, k13, raw, prob_grad, near, near2)
-
-
-def near_grads(q, qx, do, dst, pt):
-    tile = shape((PACK, DL), F32)
-    return call(
-        near_grads_kernel, (tile, tile), [VMEM] * 5,
-        flops=2 * ROWS * KEYS * DL, moved=4 << 20, name="near_grads",
-    )(q, qx, do, dst, pt)
-
-
-def queries(dst, keys, rot2):
-    outs = (shape((ROWS, DL)), shape((TOK, HEADS * DR)))
-    return call(
-        queries_kernel, outs, [VMEM] * 3, scratch=[pltpu.VMEM((ROWS, 2 * DR), F32)],
-        flops=2 * ROWS * KEYS * DL, moved=4 << 20, name="queries",
-    )(dst, keys, rot2)
-
-
-def relay(f2, r13):
-    return call(relay_kernel, shape((PACK, DL)), [VMEM] * 2, moved=600000, name="relay")(f2, r13)
-
-
-def total(g0, r13, r2, order):
-    return call(
-        total_kernel, shape((TOK, DL + DR)), [VMEM] * 3 + [HBM], moved=1 << 20, name="total"
-    )(g0, r13, r2, order)
+    )(low, q, qx, do, k1, k3, raw, prob_grad, near, near2)
+
+
+def queries(q, qx, do, dst, pt, keys, rot2):
+    outs = (shape((ROWS, DL)), shape((TOK, HEADS * DR)), shape((PACK, DL), F32))
+    return call(
+        queries_kernel, outs, [VMEM] * 7, scratch=[pltpu.VMEM((ROWS, 2 * DR), F32)],
+        flops=2 * ROWS * KEYS * DL * 2, moved=6 << 20, name="queries",
+    )(q, qx, do, dst, pt, keys, rot2)
+
+
+def total(g0, r1, r2, r3):
+    return call(
+        total_kernel, shape((TOK, DL + DR)), [VMEM] * 4, moved=1 << 20, name="total"
+    )(g0, r1, r2, r3)
 
 
 def head_sum(blocks):
@@ -320,16 +291,13 @@
     q = query_latent.reshape(ROWS, DL)
     do = out_grad.reshape(ROWS, DL)
     own = pack(in_hbm(latents), in_hbm(key_rotary.T))
-    k2 = shifted(own, "tok", 2)
+    k1, k3, k2 = [shifted(own, "tok", distance) for distance in (1, 3, 2)]
     q, do, qx, low = row_setup(doc_lengths, shard, in_hbm(q), in_hbm(do), query_rotary)
-    k13 = shifted(pair_up(own, k2, low), "tok", 1)
     raw, prob_grad, near, near2 = near_scores(q, qx, do, own, k2)
-    f13, dst, pt, keys, rot2 = scores(low, q, qx, do, k13, raw, prob_grad, near, near2)
-    r13 = shifted(f13, "tok", -1)
-    f2, g0 = near_grads(q, qx, do, dst, pt)
-    r2 = shifted(relay(f2, r13), "tok", -2)
-    dq, dqr = queries(dst, keys, rot2)
-    blocks = total(g0, r13, r2, in_hbm(dqr)).reshape(head_devices, TOK // head_devices, DL + DR)
+    f3, f2, f1, dst, pt, keys, rot2 = scores(low, q, qx, do, k1, k3, raw, prob_grad, near, near2)
+    r1, r2, r3 = [shifted(f, "tok", -d) for d, f in ((1, f1), (2, f2), (3, f3))]
+    dq, dqr, g0 = queries(q, qx, do, dst, pt, keys, rot2)
+    blocks = total(g0, r1, r2, r3).reshape(head_devices, TOK // head_devices, DL + DR)
     blocks = lax.all_to_all(blocks, "head", split_axis=0, concat_axis=0, tiled=True)
     grad_latents, grad_key_rotary = head_sum(blocks)
     return dq.reshape(TOK, HEADS, DL), dqr, grad_latents, grad_key_rotary

time: 73 us -> 71.5 us (0.979)
  the two profiles are of different devices: /device:TPU:57 before, /device:TPU:30 now
where the time goes in v4:
time: 71.5 us; the launch traced here: 71.1 us
  blocking collectives  34.2 us (48%)
  starting transfers between devices  16.7 us (23%)
  Pallas kernels  10.4 us (15%)
  waiting for transfers between devices  8.46 us (12%)
  between operations  0.77 us (1%)
    all_to_all x1, blocking collectives, body(): lax.all_to_all(blocks, 'head', split_axis=0, concat_axis=0, tiled=True)  34.2 us
    ppermute x6, starting transfers between devices, shifted(): return lax.ppermute(block, axis, route)  16.7 us
    ppermute x6, waiting for transfers between devices, shifted(): return lax.ppermute(block, axis, route)  8.46 us
    pallas_call x1, Pallas kernels, scores(): call(scores_kernel, outs, [VMEM] * 10, flops=2 * ROWS * KEYS * DL * 2, mo...  3.27 us
    pallas_call x1, Pallas kernels, queries(): call(queries_kernel, outs, [VMEM] * 7, scratch=[pltpu.VMEM((ROWS, 2 * DR)...  2.33 us
    pallas_call x1, Pallas kernels, row_setup(): call(rows_kernel, outs, [SMEM, SMEM, HBM, HBM, VMEM], scratch=[pltpu.VMEM...  2.1 us
  transfers between devices with their start and end apart: 6, of which 3 were waited for; matrix products, arithmetic and copies ran while one was open for 0% of the time, Pallas kernels for 7%

profile of v4, /device:TPU:30, one launch (start us, length us, event | category | flops | bytes accessed | tf_op | source)
XLA Modules:
  0.0 71.1 jit_solution(8783382620174988220)
XLA Ops:
  0.6 0.0 copy-start
  0.6 1.0 %pack.1.own_ref = bf16[144,512]{1,0:T(8,128)(2,1)S(1)} custom-call(bf16[128,512]{1,0:T(8,128)(2,1)} %lat_ref.1, bf16[64,128]{1,0:T(8,128)(2,1)} %bitcast.9), custom_call_target="tpu_custom_call" | custom-call | bytes 300000 | tf_op jit(solution)/shard_map/pack/pallas_call | solution.py:225
  1.6 4.7 %collective-permute-start.2 = (bf16[144,512]{1,0:T(8,128)(2,1)S(1)}, bf16[144,512]{1,0:T(8,128)(2,1)S(1)}, u32[]{:S(2)}, u32[]{:S(2)}) collective-permute-start(bf16[144,512]{1,0:T(8,128)(2,1)S(1)} %pack.1.own_ref), channel_id=1, source_target_pairs={{0,32},{16,48},{32,64},{48,80},{64,96},{80,112},{96,128},{112,144}... | collective-permute-start | bytes 442376 | tf_op jit(solution)/shard_map/ppermute | solution.py:285
  6.3 1.9 %collective-permute-start.1 = (bf16[144,512]{1,0:T(8,128)(2,1)S(1)}, bf16[144,512]{1,0:T(8,128)(2,1)S(1)}, u32[]{:S(2)}, u32[]{:S(2)}) collective-permute-start(bf16[144,512]{1,0:T(8,128)(2,1)S(1)} %pack.1.own_ref), channel_id=1, source_target_pairs={{0,48},{16,64},{32,80},{48,96},{64,112},{80,128},{96,144},{112,160... | collective-permute-start | bytes 442376 | tf_op jit(solution)/shard_map/ppermute | solution.py:285
  8.3 2.8 %collective-permute-start = (bf16[144,512]{1,0:T(8,128)(2,1)S(1)}, bf16[144,512]{1,0:T(8,128)(2,1)S(1)}, u32[]{:S(2)}, u32[]{:S(2)}) collective-permute-start(bf16[144,512]{1,0:T(8,128)(2,1)S(1)} %pack.1.own_ref), channel_id=1, source_target_pairs={{0,16},{16,32},{32,48},{48,64},{64,80},{80,96},{96,112},{112,128},... | collective-permute-start | bytes 442376 | tf_op jit(solution)/shard_map/ppermute | solution.py:285
  11.1 0.0 copy-start.1
  11.1 0.0 copy-done
  11.1 0.6 copy-done.1
  11.7 2.1 %row_setup.1 = (bf16[1024,512]{1,0:T(8,128)(2,1)S(1)}, bf16[1024,512]{1,0:T(8,128)(2,1)S(1)}, bf16[1024,128]{1,0:T(8,128)(2,1)S(1)}, s32[1,1024]{1,0:T(1,128)S(1)}) custom-call(s32[33]{0:T(128)S(1)} %copy-done.1, s32[1]{0:T(128)} %bitcast.shard_ref, bf16[1024,512]{1,0:T(8,128)(2,1)} %bitcast.7, bf16[1024,512]{1,0:T(8,128)(2,1)} %bitcast.8, ...), custom_call_target="tpu_custom_call" | custom-call | bytes 4194304 | tf_op jit(solution)/shard_map/row_setup/pallas_call | solution.py:233
  13.8 0.0 collective-permute-done.2.k2_ref
  13.9 0.9 %near_scores.1 = (f32[256,1024]{1,0:T(8,128)S(1)}, f32[256,1024]{1,0:T(8,128)S(1)}, bf16[256,512]{1,0:T(8,128)(2,1)S(1)}, bf16[256,128]{1,0:T(8,128)(2,1)S(1)}) custom-call(bf16[1024,512]{1,0:T(8,128)(2,1)S(1)} %get-tuple-element.24.q_ref, bf16[1024,128]{1,0:T(8,128)(2,1)S(1)} %get-tuple-element.25.qx_ref, bf16[1024,512]{1,0:T(8,128)(2,1)S(1)} %get-tuple-element.26.do_ref, ...), custom_call_target="tpu_custom_call" | custom-call | flops 536870912 | bytes 4194304 | tf_op jit(solution)/shard_map/near_scores/pallas_call | solution.py:244
  14.8 0.0 collective-permute-done.1.k3_ref
  14.8 2.5 %collective-permute-done.k1_ref = bf16[144,512]{1,0:T(8,128)(2,1)S(1)} collective-permute-done((bf16[144,512]{1,0:T(8,128)(2,1)S(1)}, bf16[144,512]{1,0:T(8,128)(2,1)S(1)}, u32[]{:S(2)}, u32[]{:S(2)}) %collective-permute-start) | collective-permute-done | bytes 147488 | tf_op jit(solution)/shard_map/ppermute | solution.py:285
  17.3 3.3 %scores.1 = (bf16[144,512]{1,0:T(8,128)(2,1)S(1)}, bf16[144,512]{1,0:T(8,128)(2,1)S(1)}, bf16[144,512]{1,0:T(8,128)(2,1)S(1)}, bf16[512,1024]{1,0:T(8,128)(2,1)S...) custom-call(s32[1,1024]{1,0:T(1,128)S(1)} %get-tuple-element.27.low_ref, ...), custom_call_target="tpu_custom_call" | custom-call | flops 1073741824 | bytes 6291456 | tf_op jit(solution)/shard_map/scores/pallas_call | solution.py:255
  20.6 1.9 %collective-permute-start.3 = (bf16[144,512]{1,0:T(8,128)(2,1)S(1)}, bf16[144,512]{1,0:T(8,128)(2,1)S(1)}, u32[]{:S(2)}, u32[]{:S(2)}) collective-permute-start(bf16[144,512]{1,0:T(8,128)(2,1)S(1)} %get-tuple-element.39), channel_id=1, source_target_pairs={{16,0},{32,16},{48,32},{64,48},{80,64},{96,80},{112,96},{128,112},... | collective-permute-start | bytes 442376 | tf_op jit(solution)/shard_map/ppermute | solution.py:285
  22.5 1.9 %collective-permute-start.4 = (bf16[144,512]{1,0:T(8,128)(2,1)S(1)}, bf16[144,512]{1,0:T(8,128)(2,1)S(1)}, u32[]{:S(2)}, u32[]{:S(2)}) collective-permute-start(bf16[144,512]{1,0:T(8,128)(2,1)S(1)} %get-tuple-element.40), channel_id=1, source_target_pairs={{32,0},{48,16},{64,32},{80,48},{96,64},{112,80},{128,96},{144,112}... | collective-permute-start | bytes 442376 | tf_op jit(solution)/shard_map/ppermute | solution.py:285
  24.4 3.4 %collective-permute-start.5 = (bf16[144,512]{1,0:T(8,128)(2,1)S(1)}, bf16[144,512]{1,0:T(8,128)(2,1)S(1)}, u32[]{:S(2)}, u32[]{:S(2)}) collective-permute-start(bf16[144,512]{1,0:T(8,128)(2,1)S(1)} %get-tuple-element.41), channel_id=1, source_target_pairs={{48,0},{64,16},{80,32},{96,48},{112,64},{128,80},{144,96},{160,112... | collective-permute-start | bytes 442376 | tf_op jit(solution)/shard_map/ppermute | solution.py:285
  27.8 2.3 %queries.1 = (bf16[1024,512]{1,0:T(8,128)(2,1)}, bf16[128,512]{1,0:T(8,128)(2,1)}, f32[144,512]{1,0:T(8,128)S(1)}) custom-call(bf16[1024,512]{1,0:T(8,128)(2,1)S(1)} %get-tuple-element.24.q_ref, bf16[1024,128]{1,0:T(8,128)(2,1)S(1)} %get-tuple-element.25.qx_ref, bf16[1024,512]{1,0:T(8,128)(2,1)S(1)} %get-tuple-element.26.do_ref, ...), custom_call_target="tpu_custom_call" | custom-call | flops 1073741824 | bytes 6291456 | tf_op jit(solution)/shard_map/queries/pallas_call | solution.py:263
  30.2 0.0 collective-permute-done.3.r1_ref
  30.2 2.2 %collective-permute-done.4.r2_ref = bf16[144,512]{1,0:T(8,128)(2,1)S(1)} collective-permute-done((bf16[144,512]{1,0:T(8,128)(2,1)S(1)}, bf16[144,512]{1,0:T(8,128)(2,1)S(1)}, u32[]{:S(2)}, u32[]{:S(2)}) %collective-permute-start.4) | collective-permute-done | bytes 147488 | tf_op jit(solution)/shard_map/ppermute | solution.py:285
  32.3 3.8 %collective-permute-done.5.r3_ref = bf16[144,512]{1,0:T(8,128)(2,1)S(1)} collective-permute-done((bf16[144,512]{1,0:T(8,128)(2,1)S(1)}, bf16[144,512]{1,0:T(8,128)(2,1)S(1)}, u32[]{:S(2)}, u32[]{:S(2)}) %collective-permute-start.5) | collective-permute-done | bytes 147488 | tf_op jit(solution)/shard_map/ppermute | solution.py:285
  36.1 0.2 total.1
  36.3 34.2 %all_to_all.5.blocks_ref = bf16[16,8,576]{2,1,0:T(8,128)(2,1)S(1)} all-to-all(bf16[16,8,576]{2,1,0:T(8,128)(2,1)S(1)} %bitcast.6), channel_id=1, replica_groups=mesh['tok'=64,'head'=16] {'head'}, dimensions={0} | all-to-all | bytes 294912 | tf_op jit(solution)/shard_map/all_to_all | solution.py:301
  70.5 0.6 head_sum.1
Async XLA Ops:
  0.6 10.5 %copy-start = (bf16[128,512]{1,0:T(8,128)(2,1)S(1)}, bf16[128,512]{1,0:T(8,128)(2,1)}, u32[]{:S(2)}) copy-start(bf16[128,512]{1,0:T(8,128)(2,1)} %qr_ref.1) | copy-start | bytes 393220
  1.6 12.2 %collective-permute-start.2 = (bf16[144,512]{1,0:T(8,128)(2,1)S(1)}, bf16[144,512]{1,0:T(8,128)(2,1)S(1)}, u32[]{:S(2)}, u32[]{:S(2)}) collective-permute-start(bf16[144,512]{1,0:T(8,128)(2,1)S(1)} %pack.1.own_ref), channel_id=1, source_target_pairs={{0,32},{16,48},{32,64},{48,80},{64,96},{80,112},{96,128},{112,144}... | collective-permute-start | bytes 442376 | tf_op jit(solution)/shard_map/ppermute | solution.py:285
  6.3 8.4 %collective-permute-start.1 = (bf16[144,512]{1,0:T(8,128)(2,1)S(1)}, bf16[144,512]{1,0:T(8,128)(2,1)S(1)}, u32[]{:S(2)}, u32[]{:S(2)}) collective-permute-start(bf16[144,512]{1,0:T(8,128)(2,1)S(1)} %pack.1.own_ref), channel_id=1, source_target_pairs={{0,48},{16,64},{32,80},{48,96},{64,112},{80,128},{96,144},{112,160... | collective-permute-start | bytes 442376 | tf_op jit(solution)/shard_map/ppermute | solution.py:285
  8.3 9.0 %collective-permute-start = (bf16[144,512]{1,0:T(8,128)(2,1)S(1)}, bf16[144,512]{1,0:T(8,128)(2,1)S(1)}, u32[]{:S(2)}, u32[]{:S(2)}) collective-permute-start(bf16[144,512]{1,0:T(8,128)(2,1)S(1)} %pack.1.own_ref), channel_id=1, source_target_pairs={{0,16},{16,32},{32,48},{48,64},{64,80},{80,96},{96,112},{112,128},... | collective-permute-start | bytes 442376 | tf_op jit(solution)/shard_map/ppermute | solution.py:285
  11.1 0.7 copy-start.1
  20.6 9.6 %collective-permute-start.3 = (bf16[144,512]{1,0:T(8,128)(2,1)S(1)}, bf16[144,512]{1,0:T(8,128)(2,1)S(1)}, u32[]{:S(2)}, u32[]{:S(2)}) collective-permute-start(bf16[144,512]{1,0:T(8,128)(2,1)S(1)} %get-tuple-element.39), channel_id=1, source_target_pairs={{16,0},{32,16},{48,32},{64,48},{80,64},{96,80},{112,96},{128,112},... | collective-permute-start | bytes 442376 | tf_op jit(solution)/shard_map/ppermute | solution.py:285
  22.5 9.8 %collective-permute-start.4 = (bf16[144,512]{1,0:T(8,128)(2,1)S(1)}, bf16[144,512]{1,0:T(8,128)(2,1)S(1)}, u32[]{:S(2)}, u32[]{:S(2)}) collective-permute-start(bf16[144,512]{1,0:T(8,128)(2,1)S(1)} %get-tuple-element.40), channel_id=1, source_target_pairs={{32,0},{48,16},{64,32},{80,48},{96,64},{112,80},{128,96},{144,112}... | collective-permute-start | bytes 442376 | tf_op jit(solution)/shard_map/ppermute | solution.py:285
  24.4 11.7 %collective-permute-start.5 = (bf16[144,512]{1,0:T(8,128)(2,1)S(1)}, bf16[144,512]{1,0:T(8,128)(2,1)S(1)}, u32[]{:S(2)}, u32[]{:S(2)}) collective-permute-start(bf16[144,512]{1,0:T(8,128)(2,1)S(1)} %get-tuple-element.41), channel_id=1, source_target_pairs={{48,0},{64,16},{80,32},{96,48},{112,64},{128,80},{144,96},{160,112... | collective-permute-start | bytes 442376 | tf_op jit(solution)/shard_map/ppermute | solution.py:285

commit v5 on v4

--- a/solution.py
+++ b/solution.py
@@ -22,6 +22,7 @@
 PACK = TOK + TOK * DR // DL
 CHUNK = 256
 HALF = KEYS // 2
+FETCHES = 4
 
 F32 = jnp.float32
 BF16 = jnp.bfloat16
@@ -69,13 +70,24 @@
     return (lane >= DR) == (head % 2 == 1)
 
 
+def shard_index():
+    return lax.axis_index("tok").astype(jnp.int32)
+
+
 def rows_kernel(
-    lens_ref, shard_ref, q_ref, do_ref, qr_ref, qv_ref, dov_ref, qx_ref, low_ref, qx32_ref, sems
+    lens_ref, q_ref, do_ref, qr_ref, qv_ref, dov_ref, qx_ref, low_ref, lens_smem, qx32_ref, sems
 ):
-    q_copy = pltpu.make_async_copy(q_ref, qv_ref, sems.at[0])
-    do_copy = pltpu.make_async_copy(do_ref, dov_ref, sems.at[1])
-    q_copy.start()
-    do_copy.start()
+    copies = []
+    for i in range(FETCHES):
+        part = pl.ds(i * ROWS // FETCHES, ROWS // FETCHES)
+        copies.append(pltpu.make_async_copy(q_ref.at[part, :], qv_ref.at[part, :], sems.at[2 * i]))
+        copies.append(
+            pltpu.make_async_copy(do_ref.at[part, :], dov_ref.at[part, :], sems.at[2 * i + 1])
+        )
+    lens_copy = pltpu.make_async_copy(lens_ref, lens_smem, sems.at[2 * FETCHES])
+    lens_copy.start()
+    for copy in copies:
+        copy.start()
     for head in range(HEADS):
         pair = qr_ref[:, (head // 2) * 2 * DR : (head // 2 + 1) * 2 * DR].astype(F32)
         qx32_ref[pl.ds(head, TOK, stride=HEADS), :] = jnp.where(
@@ -84,13 +96,14 @@
     qx_ref[...] = qx32_ref[...].astype(BF16)
     high = lax.broadcasted_iota(jnp.int32, (1, ROWS), 1) // HEADS + FAR
     low = jnp.zeros((1, ROWS), jnp.int32)
-    start = (SPAN - shard_ref[0]) * TOK
-    for doc in range(lens_ref.shape[0]):
+    start = (SPAN - shard_index()) * TOK
+    lens_copy.wait()
+    for doc in range(lens_smem.shape[0]):
         low = jnp.where(high >= start, start, low)
-        start = start + lens_ref[doc]
+        start = start + lens_smem[doc]
     low_ref[...] = low
-    q_copy.wait()
-    do_copy.wait()
+    for copy in copies:
+        copy.wait()
 
 
 def load_keys(ref, slot, keys_ref, rot2_ref):
@@ -184,9 +197,9 @@
         ).astype(BF16)
 
 
-def total_kernel(g0_ref, r1_ref, r2_ref, r3_ref, out_ref):
+def total_kernel(g0_ref, r3_ref, r2_ref, r1_ref, out_ref):
     total = g0_ref[...]
-    for ref in (r1_ref, r2_ref, r3_ref):
+    for ref in (r3_ref, r2_ref, r1_ref):
         total = total + ref[...].astype(F32)
     out_ref[:, 0:DL] = total[0:TOK, :].astype(BF16)
     parts = [total[TOK:, i * TOK : (i + 1) * TOK] for i in range(DL // TOK)]
@@ -228,13 +241,17 @@
     )(latents, rotary_t)
 
 
-def row_setup(lens, shard, q, do, qr):
+def row_setup(lens, q, do, qr):
     outs = (shape((ROWS, DL)), shape((ROWS, DL)), shape((ROWS, 2 * DR)), shape((1, ROWS), jnp.int32))
     return call(
-        rows_kernel, outs, [SMEM, SMEM, HBM, HBM, VMEM],
-        scratch=[pltpu.VMEM((ROWS, 2 * DR), F32), pltpu.SemaphoreType.DMA((2,))],
+        rows_kernel, outs, [HBM, HBM, HBM, VMEM],
+        scratch=[
+            pltpu.SMEM(lens.shape, jnp.int32),
+            pltpu.VMEM((ROWS, 2 * DR), F32),
+            pltpu.SemaphoreType.DMA((2 * FETCHES + 1,)),
+        ],
         moved=4 << 20, name="row_setup",
-    )(lens, shard, q, do, qr)
+    )(lens, q, do, qr)
 
 
 def near_scores(q, qx, do, own, k2):
@@ -266,10 +283,10 @@
     )(q, qx, do, dst, pt, keys, rot2)
 
 
-def total(g0, r1, r2, r3):
+def total(g0, r3, r2, r1):
     return call(
         total_kernel, shape((TOK, DL + DR)), [VMEM] * 4, moved=1 << 20, name="total"
-    )(g0, r1, r2, r3)
+    )(g0, r3, r2, r1)
 
 
 def head_sum(blocks):
@@ -287,17 +304,16 @@
 
 def body(query_latent, query_rotary, latents, key_rotary, out_grad, doc_lengths):
     head_devices = lax.axis_size("head")
-    shard = jnp.reshape(lax.axis_index("tok"), (1,)).astype(jnp.int32)
     q = query_latent.reshape(ROWS, DL)
     do = out_grad.reshape(ROWS, DL)
     own = pack(in_hbm(latents), in_hbm(key_rotary.T))
     k1, k3, k2 = [shifted(own, "tok", distance) for distance in (1, 3, 2)]
-    q, do, qx, low = row_setup(doc_lengths, shard, in_hbm(q), in_hbm(do), query_rotary)
+    q, do, qx, low = row_setup(in_hbm(doc_lengths), in_hbm(q), in_hbm(do), query_rotary)
     raw, prob_grad, near, near2 = near_scores(q, qx, do, own, k2)
     f3, f2, f1, dst, pt, keys, rot2 = scores(low, q, qx, do, k1, k3, raw, prob_grad, near, near2)
-    r1, r2, r3 = [shifted(f, "tok", -d) for d, f in ((1, f1), (2, f2), (3, f3))]
+    r3, r2, r1 = [shifted(f, "tok", -d) for d, f in ((3, f3), (2, f2), (1, f1))]
     dq, dqr, g0 = queries(q, qx, do, dst, pt, keys, rot2)
-    blocks = total(g0, r1, r2, r3).reshape(head_devices, TOK // head_devices, DL + DR)
+    blocks = total(g0, r3, r2, r1).reshape(head_devices, TOK // head_devices, DL + DR)
     blocks = lax.all_to_all(blocks, "head", split_axis=0, concat_axis=0, tiled=True)
     grad_latents, grad_key_rotary = head_sum(blocks)
     return dq.reshape(TOK, HEADS, DL), dqr, grad_latents, grad_key_rotary

time: 71.5 us -> 69.2 us (0.968)
  the two profiles are of different devices: /device:TPU:30 before, /device:TPU:57 now
where the time goes in v5:
time: 69.2 us; the launch traced here: 68.2 us
  blocking collectives  32.3 us (47%)
  starting transfers between devices  18.6 us (27%)
  Pallas kernels  9.86 us (14%)
  waiting for transfers between devices  6.61 us (10%)
  between operations  0.75 us (1%)
    all_to_all x1, blocking collectives, body(): lax.all_to_all(blocks, 'head', split_axis=0, concat_axis=0, tiled=True)  32.3 us
    ppermute x6, starting transfers between devices, shifted(): return lax.ppermute(block, axis, route)  18.6 us
    ppermute x6, waiting for transfers between devices, shifted(): return lax.ppermute(block, axis, route)  6.61 us
    pallas_call x1, Pallas kernels, scores(): call(scores_kernel, outs, [VMEM] * 10, flops=2 * ROWS * KEYS * DL * 2, mo...  3.25 us
    pallas_call x1, Pallas kernels, queries(): call(queries_kernel, outs, [VMEM] * 7, scratch=[pltpu.VMEM((ROWS, 2 * DR)...  2.33 us
    pallas_call x1, Pallas kernels, row_setup(): call(rows_kernel, outs, [HBM, HBM, HBM, VMEM], scratch=[pltpu.SMEM(lens.s...  1.6 us
  transfers between devices with their start and end apart: 6, of which 4 were waited for; matrix products, arithmetic and copies ran while one was open for 0% of the time, Pallas kernels for 7%

profile of v5, /device:TPU:57, one launch (start us, length us, event | category | flops | bytes accessed | tf_op | source)
XLA Modules:
  0.0 68.2 jit_solution(2719720943761442908)
XLA Ops:
  0.6 0.0 copy-start
  0.6 1.0 %pack.1.own_ref = bf16[144,512]{1,0:T(8,128)(2,1)S(1)} custom-call(bf16[128,512]{1,0:T(8,128)(2,1)} %lat_ref.1, bf16[64,128]{1,0:T(8,128)(2,1)} %bitcast.8), custom_call_target="tpu_custom_call" | custom-call | bytes 300000 | tf_op jit(solution)/shard_map/pack/pallas_call | solution.py:238
  1.6 2.3 %collective-permute-start.2 = (bf16[144,512]{1,0:T(8,128)(2,1)S(1)}, bf16[144,512]{1,0:T(8,128)(2,1)S(1)}, u32[]{:S(2)}, u32[]{:S(2)}) collective-permute-start(bf16[144,512]{1,0:T(8,128)(2,1)S(1)} %pack.1.own_ref), channel_id=1, source_target_pairs={{0,32},{16,48},{32,64},{48,80},{64,96},{80,112},{96,128},{112,144}... | collective-permute-start | bytes 442376 | tf_op jit(solution)/shard_map/ppermute | solution.py:302
  4.0 5.1 %collective-permute-start.1 = (bf16[144,512]{1,0:T(8,128)(2,1)S(1)}, bf16[144,512]{1,0:T(8,128)(2,1)S(1)}, u32[]{:S(2)}, u32[]{:S(2)}) collective-permute-start(bf16[144,512]{1,0:T(8,128)(2,1)S(1)} %pack.1.own_ref), channel_id=1, source_target_pairs={{0,48},{16,64},{32,80},{48,96},{64,112},{80,128},{96,144},{112,160... | collective-permute-start | bytes 442376 | tf_op jit(solution)/shard_map/ppermute | solution.py:302
  9.0 1.9 %collective-permute-start = (bf16[144,512]{1,0:T(8,128)(2,1)S(1)}, bf16[144,512]{1,0:T(8,128)(2,1)S(1)}, u32[]{:S(2)}, u32[]{:S(2)}) collective-permute-start(bf16[144,512]{1,0:T(8,128)(2,1)S(1)} %pack.1.own_ref), channel_id=1, source_target_pairs={{0,16},{16,32},{32,48},{48,64},{64,80},{80,96},{96,112},{112,128},... | collective-permute-start | bytes 442376 | tf_op jit(solution)/shard_map/ppermute | solution.py:302
  11.0 0.0 copy-done
  11.0 1.6 %row_setup.1 = (bf16[1024,512]{1,0:T(8,128)(2,1)S(1)}, bf16[1024,512]{1,0:T(8,128)(2,1)S(1)}, bf16[1024,128]{1,0:T(8,128)(2,1)S(1)}, s32[1,1024]{1,0:T(1,128)S(1)}) custom-call(s32[33]{0:T(128)} %lens_ref.1, bf16[1024,512]{1,0:T(8,128)(2,1)} %bitcast.6, bf16[1024,512]{1,0:T(8,128)(2,1)} %bitcast.7, bf16[128,512]{1,0:T(8,128)(2,1)S(1)} %copy-done), custom_call_target="tpu_custom_call" | custom-call | bytes 4194304 | tf_op jit(solution)/shard_map/row_setup/pallas_call | solution.py:246
  12.6 0.0 collective-permute-done.2.k2_ref
  12.6 0.9 %near_scores.1 = (f32[256,1024]{1,0:T(8,128)S(1)}, f32[256,1024]{1,0:T(8,128)S(1)}, bf16[256,512]{1,0:T(8,128)(2,1)S(1)}, bf16[256,128]{1,0:T(8,128)(2,1)S(1)}) custom-call(bf16[1024,512]{1,0:T(8,128)(2,1)S(1)} %get-tuple-element.24.q_ref, bf16[1024,128]{1,0:T(8,128)(2,1)S(1)} %get-tuple-element.25.qx_ref, bf16[1024,512]{1,0:T(8,128)(2,1)S(1)} %get-tuple-element.26.do_ref, ...), custom_call_target="tpu_custom_call" | custom-call | flops 536870912 | bytes 4194304 | tf_op jit(solution)/shard_map/near_scores/pallas_call | solution.py:261
  13.5 0.0 collective-permute-done.1.k3_ref
  13.5 1.1 %collective-permute-done.k1_ref = bf16[144,512]{1,0:T(8,128)(2,1)S(1)} collective-permute-done((bf16[144,512]{1,0:T(8,128)(2,1)S(1)}, bf16[144,512]{1,0:T(8,128)(2,1)S(1)}, u32[]{:S(2)}, u32[]{:S(2)}) %collective-permute-start) | collective-permute-done | bytes 147488 | tf_op jit(solution)/shard_map/ppermute | solution.py:302
  14.6 3.2 %scores.1 = (bf16[144,512]{1,0:T(8,128)(2,1)S(1)}, bf16[144,512]{1,0:T(8,128)(2,1)S(1)}, bf16[144,512]{1,0:T(8,128)(2,1)S(1)}, bf16[512,1024]{1,0:T(8,128)(2,1)S...) custom-call(s32[1,1024]{1,0:T(1,128)S(1)} %get-tuple-element.27.low_ref, ...), custom_call_target="tpu_custom_call" | custom-call | flops 1073741824 | bytes 6291456 | tf_op jit(solution)/shard_map/scores/pallas_call | solution.py:272
  17.8 4.4 %collective-permute-start.3 = (bf16[144,512]{1,0:T(8,128)(2,1)S(1)}, bf16[144,512]{1,0:T(8,128)(2,1)S(1)}, u32[]{:S(2)}, u32[]{:S(2)}) collective-permute-start(bf16[144,512]{1,0:T(8,128)(2,1)S(1)} %get-tuple-element.39), channel_id=1, source_target_pairs={{48,0},{64,16},{80,32},{96,48},{112,64},{128,80},{144,96},{160,112... | collective-permute-start | bytes 442376 | tf_op jit(solution)/shard_map/ppermute | solution.py:302
  22.2 3.0 %collective-permute-start.4 = (bf16[144,512]{1,0:T(8,128)(2,1)S(1)}, bf16[144,512]{1,0:T(8,128)(2,1)S(1)}, u32[]{:S(2)}, u32[]{:S(2)}) collective-permute-start(bf16[144,512]{1,0:T(8,128)(2,1)S(1)} %get-tuple-element.40), channel_id=1, source_target_pairs={{32,0},{48,16},{64,32},{80,48},{96,64},{112,80},{128,96},{144,112}... | collective-permute-start | bytes 442376 | tf_op jit(solution)/shard_map/ppermute | solution.py:302
  25.2 1.9 %collective-permute-start.5 = (bf16[144,512]{1,0:T(8,128)(2,1)S(1)}, bf16[144,512]{1,0:T(8,128)(2,1)S(1)}, u32[]{:S(2)}, u32[]{:S(2)}) collective-permute-start(bf16[144,512]{1,0:T(8,128)(2,1)S(1)} %get-tuple-element.41), channel_id=1, source_target_pairs={{16,0},{32,16},{48,32},{64,48},{80,64},{96,80},{112,96},{128,112},... | collective-permute-start | bytes 442376 | tf_op jit(solution)/shard_map/ppermute | solution.py:302
  27.2 2.3 %queries.1 = (bf16[1024,512]{1,0:T(8,128)(2,1)}, bf16[128,512]{1,0:T(8,128)(2,1)}, f32[144,512]{1,0:T(8,128)S(1)}) custom-call(bf16[1024,512]{1,0:T(8,128)(2,1)S(1)} %get-tuple-element.24.q_ref, bf16[1024,128]{1,0:T(8,128)(2,1)S(1)} %get-tuple-element.25.qx_ref, bf16[1024,512]{1,0:T(8,128)(2,1)S(1)} %get-tuple-element.26.do_ref, ...), custom_call_target="tpu_custom_call" | custom-call | flops 1073741824 | bytes 6291456 | tf_op jit(solution)/shard_map/queries/pallas_call | solution.py:280
  29.5 0.4 collective-permute-done.3.r3_ref
  29.9 3.7 %collective-permute-done.4.r2_ref = bf16[144,512]{1,0:T(8,128)(2,1)S(1)} collective-permute-done((bf16[144,512]{1,0:T(8,128)(2,1)S(1)}, bf16[144,512]{1,0:T(8,128)(2,1)S(1)}, u32[]{:S(2)}, u32[]{:S(2)}) %collective-permute-start.4) | collective-permute-done | bytes 147488 | tf_op jit(solution)/shard_map/ppermute | solution.py:302
  33.6 1.4 %collective-permute-done.5.r1_ref = bf16[144,512]{1,0:T(8,128)(2,1)S(1)} collective-permute-done((bf16[144,512]{1,0:T(8,128)(2,1)S(1)}, bf16[144,512]{1,0:T(8,128)(2,1)S(1)}, u32[]{:S(2)}, u32[]{:S(2)}) %collective-permute-start.5) | collective-permute-done | bytes 147488 | tf_op jit(solution)/shard_map/ppermute | solution.py:302
  35.0 0.2 total.1
  35.2 32.3 %all_to_all.5.blocks_ref = bf16[16,8,576]{2,1,0:T(8,128)(2,1)S(1)} all-to-all(bf16[16,8,576]{2,1,0:T(8,128)(2,1)S(1)} %bitcast.5), channel_id=1, replica_groups=mesh['tok'=64,'head'=16] {'head'}, dimensions={0} | all-to-all | bytes 294912 | tf_op jit(solution)/shard_map/all_to_all | solution.py:317
  67.5 0.6 head_sum.1
Async XLA Ops:
  0.6 10.3 %copy-start = (bf16[128,512]{1,0:T(8,128)(2,1)S(1)}, bf16[128,512]{1,0:T(8,128)(2,1)}, u32[]{:S(2)}) copy-start(bf16[128,512]{1,0:T(8,128)(2,1)} %qr_ref.1) | copy-start | bytes 393220
  1.6 10.9 %collective-permute-start.2 = (bf16[144,512]{1,0:T(8,128)(2,1)S(1)}, bf16[144,512]{1,0:T(8,128)(2,1)S(1)}, u32[]{:S(2)}, u32[]{:S(2)}) collective-permute-start(bf16[144,512]{1,0:T(8,128)(2,1)S(1)} %pack.1.own_ref), channel_id=1, source_target_pairs={{0,32},{16,48},{32,64},{48,80},{64,96},{80,112},{96,128},{112,144}... | collective-permute-start | bytes 442376 | tf_op jit(solution)/shard_map/ppermute | solution.py:302
  4.0 9.5 %collective-permute-start.1 = (bf16[144,512]{1,0:T(8,128)(2,1)S(1)}, bf16[144,512]{1,0:T(8,128)(2,1)S(1)}, u32[]{:S(2)}, u32[]{:S(2)}) collective-permute-start(bf16[144,512]{1,0:T(8,128)(2,1)S(1)} %pack.1.own_ref), channel_id=1, source_target_pairs={{0,48},{16,64},{32,80},{48,96},{64,112},{80,128},{96,144},{112,160... | collective-permute-start | bytes 442376 | tf_op jit(solution)/shard_map/ppermute | solution.py:302
  9.0 5.5 %collective-permute-start = (bf16[144,512]{1,0:T(8,128)(2,1)S(1)}, bf16[144,512]{1,0:T(8,128)(2,1)S(1)}, u32[]{:S(2)}, u32[]{:S(2)}) collective-permute-start(bf16[144,512]{1,0:T(8,128)(2,1)S(1)} %pack.1.own_ref), channel_id=1, source_target_pairs={{0,16},{16,32},{32,48},{48,64},{64,80},{80,96},{96,112},{112,128},... | collective-permute-start | bytes 442376 | tf_op jit(solution)/shard_map/ppermute | solution.py:302
  17.8 12.1 %collective-permute-start.3 = (bf16[144,512]{1,0:T(8,128)(2,1)S(1)}, bf16[144,512]{1,0:T(8,128)(2,1)S(1)}, u32[]{:S(2)}, u32[]{:S(2)}) collective-permute-start(bf16[144,512]{1,0:T(8,128)(2,1)S(1)} %get-tuple-element.39), channel_id=1, source_target_pairs={{48,0},{64,16},{80,32},{96,48},{112,64},{128,80},{144,96},{160,112... | collective-permute-start | bytes 442376 | tf_op jit(solution)/shard_map/ppermute | solution.py:302
  22.2 11.4 %collective-permute-start.4 = (bf16[144,512]{1,0:T(8,128)(2,1)S(1)}, bf16[144,512]{1,0:T(8,128)(2,1)S(1)}, u32[]{:S(2)}, u32[]{:S(2)}) collective-permute-start(bf16[144,512]{1,0:T(8,128)(2,1)S(1)} %get-tuple-element.40), channel_id=1, source_target_pairs={{32,0},{48,16},{64,32},{80,48},{96,64},{112,80},{128,96},{144,112}... | collective-permute-start | bytes 442376 | tf_op jit(solution)/shard_map/ppermute | solution.py:302
  25.2 9.8 %collective-permute-start.5 = (bf16[144,512]{1,0:T(8,128)(2,1)S(1)}, bf16[144,512]{1,0:T(8,128)(2,1)S(1)}, u32[]{:S(2)}, u32[]{:S(2)}) collective-permute-start(bf16[144,512]{1,0:T(8,128)(2,1)S(1)} %get-tuple-element.41), channel_id=1, source_target_pairs={{16,0},{32,16},{48,32},{64,48},{80,64},{96,80},{112,96},{128,112},... | collective-permute-start | bytes 442376 | tf_op jit(solution)/shard_map/ppermute | solution.py:302

commit v6 on v5

--- a/solution.py
+++ b/solution.py
@@ -22,6 +22,7 @@
 PACK = TOK + TOK * DR // DL
 CHUNK = 256
 HALF = KEYS // 2
+BLOCK = 2 * (DL // TOK) + 1
 FETCHES = 4
 
 F32 = jnp.float32
@@ -201,16 +202,23 @@
     total = g0_ref[...]
     for ref in (r3_ref, r2_ref, r1_ref):
         total = total + ref[...].astype(F32)
-    out_ref[:, 0:DL] = total[0:TOK, :].astype(BF16)
+    groups = out_ref.shape[0]
+    for i in range(DL // TOK):
+        piece = total[0:TOK, i * TOK : (i + 1) * TOK].reshape(groups, 2, 4, TOK)
+        out_ref[:, 2 * i : 2 * i + 2, :, :] = piece.astype(BF16)
     parts = [total[TOK:, i * TOK : (i + 1) * TOK] for i in range(DL // TOK)]
-    rot = jnp.transpose(jnp.concatenate(parts + parts, axis=0))
-    out_ref[:, DL:] = rot[:, 0:DR].astype(BF16)
+    rot = jnp.transpose(jnp.concatenate(parts + parts, axis=0)).reshape(groups, 2, 4, 2 * DR)
+    lane = lax.broadcasted_iota(jnp.int32, (groups, 4, 2 * DR), 2)
+    out_ref[:, 2 * (DL // TOK), :, :] = jnp.where(lane < DR, rot[:, 0], rot[:, 1]).astype(BF16)
 
 
 def sum_kernel(blocks_ref, lat_ref, rot_ref):
     total = jnp.sum(blocks_ref[...].astype(F32), axis=0)
-    lat_ref[...] = total[:, 0:DL].astype(BF16)
-    rot_ref[...] = total[:, DL:].astype(BF16)
+    for i in range(DL // TOK):
+        rows = jnp.concatenate([total[2 * i], total[2 * i + 1]], axis=0)
+        lat_ref[:, i * TOK : (i + 1) * TOK] = rows.astype(BF16)
+    last = total[2 * (DL // TOK)]
+    rot_ref[...] = jnp.concatenate([last[:, 0:DR], last[:, DR:]], axis=0).astype(BF16)
 
 
 def shape(dims, dtype=BF16):
@@ -283,14 +291,14 @@
     )(q, qx, do, dst, pt, keys, rot2)
 
 
-def total(g0, r3, r2, r1):
-    return call(
-        total_kernel, shape((TOK, DL + DR)), [VMEM] * 4, moved=1 << 20, name="total"
+def total(g0, r3, r2, r1, groups):
+    return call(
+        total_kernel, shape((groups, BLOCK, 4, TOK)), [VMEM] * 4, moved=1 << 20, name="total"
     )(g0, r3, r2, r1)
 
 
 def head_sum(blocks):
-    rows = blocks.shape[1]
+    rows = TOK // blocks.shape[0]
     return call(
         sum_kernel, (shape((rows, DL)), shape((rows, DR))), [VMEM], moved=200000, name="head_sum"
     )(blocks)
@@ -307,13 +315,13 @@
     q = query_latent.reshape(ROWS, DL)
     do = out_grad.reshape(ROWS, DL)
     own = pack(in_hbm(latents), in_hbm(key_rotary.T))
-    k1, k3, k2 = [shifted(own, "tok", distance) for distance in (1, 3, 2)]
+    k1, k2, k3 = [shifted(own, "tok", distance) for distance in (1, 2, 3)]
     q, do, qx, low = row_setup(in_hbm(doc_lengths), in_hbm(q), in_hbm(do), query_rotary)
     raw, prob_grad, near, near2 = near_scores(q, qx, do, own, k2)
     f3, f2, f1, dst, pt, keys, rot2 = scores(low, q, qx, do, k1, k3, raw, prob_grad, near, near2)
     r3, r2, r1 = [shifted(f, "tok", -d) for d, f in ((3, f3), (2, f2), (1, f1))]
     dq, dqr, g0 = queries(q, qx, do, dst, pt, keys, rot2)
-    blocks = total(g0, r3, r2, r1).reshape(head_devices, TOK // head_devices, DL + DR)
+    blocks = total(g0, r3, r2, r1, head_devices)
     blocks = lax.all_to_all(blocks, "head", split_axis=0, concat_axis=0, tiled=True)
     grad_latents, grad_key_rotary = head_sum(blocks)
     return dq.reshape(TOK, HEADS, DL), dqr, grad_latents, grad_key_rotary

time: 69.2 us -> 69.1 us (level)
  the two profiles are of different devices: /device:TPU:57 before, /device:TPU:68 now
where the time goes in v6:
time: 69.1 us; the launch traced here: 68.8 us
  blocking collectives  33.9 us (49%)
  starting transfers between devices  18.6 us (27%)
  Pallas kernels  9.99 us (14%)
  waiting for transfers between devices  5.51 us (8%)
  between operations  0.74 us (1%)
    all_to_all x1, blocking collectives, body(): lax.all_to_all(blocks, 'head', split_axis=0, concat_axis=0, tiled=True)  33.9 us
    ppermute x6, starting transfers between devices, shifted(): return lax.ppermute(block, axis, route)  18.6 us
    ppermute x6, waiting for transfers between devices, shifted(): return lax.ppermute(block, axis, route)  5.51 us
    pallas_call x1, Pallas kernels, scores(): call(scores_kernel, outs, [VMEM] * 10, flops=2 * ROWS * KEYS * DL * 2, mo...  3.24 us
    pallas_call x1, Pallas kernels, queries(): call(queries_kernel, outs, [VMEM] * 7, scratch=[pltpu.VMEM((ROWS, 2 * DR)...  2.33 us
    pallas_call x1, Pallas kernels, row_setup(): call(rows_kernel, outs, [HBM, HBM, HBM, VMEM], scratch=[pltpu.SMEM(lens.s...  1.6 us
  transfers between devices with their start and end apart: 6, of which 4 were waited for; matrix products, arithmetic and copies ran while one was open for 0% of the time, Pallas kernels for 7%

profile of v6, /device:TPU:68, one launch (start us, length us, event | category | flops | bytes accessed | tf_op | source)
XLA Modules:
  0.0 68.8 jit_solution(8252927064527592076)
XLA Ops:
  0.6 0.0 copy-start
  0.6 1.0 %pack.1.own_ref = bf16[144,512]{1,0:T(8,128)(2,1)S(1)} custom-call(bf16[128,512]{1,0:T(8,128)(2,1)} %lat_ref.1, bf16[64,128]{1,0:T(8,128)(2,1)} %bitcast.6), custom_call_target="tpu_custom_call" | custom-call | bytes 300000 | tf_op jit(solution)/shard_map/pack/pallas_call | solution.py:246
  1.6 3.5 %collective-permute-start.2 = (bf16[144,512]{1,0:T(8,128)(2,1)S(1)}, bf16[144,512]{1,0:T(8,128)(2,1)S(1)}, u32[]{:S(2)}, u32[]{:S(2)}) collective-permute-start(bf16[144,512]{1,0:T(8,128)(2,1)S(1)} %pack.1.own_ref), channel_id=1, source_target_pairs={{0,32},{16,48},{32,64},{48,80},{64,96},{80,112},{96,128},{112,144}... | collective-permute-start | bytes 442376 | tf_op jit(solution)/shard_map/ppermute | solution.py:310
  5.1 2.6 %collective-permute-start.1 = (bf16[144,512]{1,0:T(8,128)(2,1)S(1)}, bf16[144,512]{1,0:T(8,128)(2,1)S(1)}, u32[]{:S(2)}, u32[]{:S(2)}) collective-permute-start(bf16[144,512]{1,0:T(8,128)(2,1)S(1)} %pack.1.own_ref), channel_id=1, source_target_pairs={{0,48},{16,64},{32,80},{48,96},{64,112},{80,128},{96,144},{112,160... | collective-permute-start | bytes 442376 | tf_op jit(solution)/shard_map/ppermute | solution.py:310
  7.8 3.9 %collective-permute-start = (bf16[144,512]{1,0:T(8,128)(2,1)S(1)}, bf16[144,512]{1,0:T(8,128)(2,1)S(1)}, u32[]{:S(2)}, u32[]{:S(2)}) collective-permute-start(bf16[144,512]{1,0:T(8,128)(2,1)S(1)} %pack.1.own_ref), channel_id=1, source_target_pairs={{0,16},{16,32},{32,48},{48,64},{64,80},{80,96},{96,112},{112,128},... | collective-permute-start | bytes 442376 | tf_op jit(solution)/shard_map/ppermute | solution.py:310
  11.7 0.0 copy-done
  11.7 1.6 %row_setup.1 = (bf16[1024,512]{1,0:T(8,128)(2,1)S(1)}, bf16[1024,512]{1,0:T(8,128)(2,1)S(1)}, bf16[1024,128]{1,0:T(8,128)(2,1)S(1)}, s32[1,1024]{1,0:T(1,128)S(1)}) custom-call(s32[33]{0:T(128)} %lens_ref.1, bf16[1024,512]{1,0:T(8,128)(2,1)} %bitcast.4, bf16[1024,512]{1,0:T(8,128)(2,1)} %bitcast.5, bf16[128,512]{1,0:T(8,128)(2,1)S(1)} %copy-done), custom_call_target="tpu_custom_call" | custom-call | bytes 4194304 | tf_op jit(solution)/shard_map/row_setup/pallas_call | solution.py:254
  13.3 0.0 collective-permute-done.2.k2_ref
  13.3 0.9 %near_scores.1 = (f32[256,1024]{1,0:T(8,128)S(1)}, f32[256,1024]{1,0:T(8,128)S(1)}, bf16[256,512]{1,0:T(8,128)(2,1)S(1)}, bf16[256,128]{1,0:T(8,128)(2,1)S(1)}) custom-call(bf16[1024,512]{1,0:T(8,128)(2,1)S(1)} %get-tuple-element.24.q_ref, bf16[1024,128]{1,0:T(8,128)(2,1)S(1)} %get-tuple-element.25.qx_ref, bf16[1024,512]{1,0:T(8,128)(2,1)S(1)} %get-tuple-element.26.do_ref, ...), custom_call_target="tpu_custom_call" | custom-call | flops 536870912 | bytes 4194304 | tf_op jit(solution)/shard_map/near_scores/pallas_call | solution.py:269
  14.2 2.1 %collective-permute-done.1.k3_ref = bf16[144,512]{1,0:T(8,128)(2,1)S(1)} collective-permute-done((bf16[144,512]{1,0:T(8,128)(2,1)S(1)}, bf16[144,512]{1,0:T(8,128)(2,1)S(1)}, u32[]{:S(2)}, u32[]{:S(2)}) %collective-permute-start.1) | collective-permute-done | bytes 147488 | tf_op jit(solution)/shard_map/ppermute | solution.py:310
  16.3 1.9 %collective-permute-done.k1_ref = bf16[144,512]{1,0:T(8,128)(2,1)S(1)} collective-permute-done((bf16[144,512]{1,0:T(8,128)(2,1)S(1)}, bf16[144,512]{1,0:T(8,128)(2,1)S(1)}, u32[]{:S(2)}, u32[]{:S(2)}) %collective-permute-start) | collective-permute-done | bytes 147488 | tf_op jit(solution)/shard_map/ppermute | solution.py:310
  18.2 3.2 %scores.1 = (bf16[144,512]{1,0:T(8,128)(2,1)S(1)}, bf16[144,512]{1,0:T(8,128)(2,1)S(1)}, bf16[144,512]{1,0:T(8,128)(2,1)S(1)}, bf16[512,1024]{1,0:T(8,128)(2,1)S...) custom-call(s32[1,1024]{1,0:T(1,128)S(1)} %get-tuple-element.27.low_ref, ...), custom_call_target="tpu_custom_call" | custom-call | flops 1073741824 | bytes 6291456 | tf_op jit(solution)/shard_map/scores/pallas_call | solution.py:280
  21.4 1.9 %collective-permute-start.3 = (bf16[144,512]{1,0:T(8,128)(2,1)S(1)}, bf16[144,512]{1,0:T(8,128)(2,1)S(1)}, u32[]{:S(2)}, u32[]{:S(2)}) collective-permute-start(bf16[144,512]{1,0:T(8,128)(2,1)S(1)} %get-tuple-element.39), channel_id=1, source_target_pairs={{48,0},{64,16},{80,32},{96,48},{112,64},{128,80},{144,96},{160,112... | collective-permute-start | bytes 442376 | tf_op jit(solution)/shard_map/ppermute | solution.py:310
  23.4 2.7 %collective-permute-start.4 = (bf16[144,512]{1,0:T(8,128)(2,1)S(1)}, bf16[144,512]{1,0:T(8,128)(2,1)S(1)}, u32[]{:S(2)}, u32[]{:S(2)}) collective-permute-start(bf16[144,512]{1,0:T(8,128)(2,1)S(1)} %get-tuple-element.40), channel_id=1, source_target_pairs={{32,0},{48,16},{64,32},{80,48},{96,64},{112,80},{128,96},{144,112}... | collective-permute-start | bytes 442376 | tf_op jit(solution)/shard_map/ppermute | solution.py:310
  26.0 4.0 %collective-permute-start.5 = (bf16[144,512]{1,0:T(8,128)(2,1)S(1)}, bf16[144,512]{1,0:T(8,128)(2,1)S(1)}, u32[]{:S(2)}, u32[]{:S(2)}) collective-permute-start(bf16[144,512]{1,0:T(8,128)(2,1)S(1)} %get-tuple-element.41), channel_id=1, source_target_pairs={{16,0},{32,16},{48,32},{64,48},{80,64},{96,80},{112,96},{128,112},... | collective-permute-start | bytes 442376 | tf_op jit(solution)/shard_map/ppermute | solution.py:310
  30.0 2.3 %queries.1 = (bf16[1024,512]{1,0:T(8,128)(2,1)}, bf16[128,512]{1,0:T(8,128)(2,1)}, f32[144,512]{1,0:T(8,128)S(1)}) custom-call(bf16[1024,512]{1,0:T(8,128)(2,1)S(1)} %get-tuple-element.24.q_ref, bf16[1024,128]{1,0:T(8,128)(2,1)S(1)} %get-tuple-element.25.qx_ref, bf16[1024,512]{1,0:T(8,128)(2,1)S(1)} %get-tuple-element.26.do_ref, ...), custom_call_target="tpu_custom_call" | custom-call | flops 1073741824 | bytes 6291456 | tf_op jit(solution)/shard_map/queries/pallas_call | solution.py:288
  32.4 0.0 collective-permute-done.3.r3_ref
  32.4 0.6 collective-permute-done.4.r2_ref
  33.0 0.9 %collective-permute-done.5.r1_ref = bf16[144,512]{1,0:T(8,128)(2,1)S(1)} collective-permute-done((bf16[144,512]{1,0:T(8,128)(2,1)S(1)}, bf16[144,512]{1,0:T(8,128)(2,1)S(1)}, u32[]{:S(2)}, u32[]{:S(2)}) %collective-permute-start.5) | collective-permute-done | bytes 147488 | tf_op jit(solution)/shard_map/ppermute | solution.py:310
  33.9 0.2 total.1
  34.1 33.9 %all_to_all.5.blocks_ref = bf16[16,9,4,128]{3,2,1,0:T(4,128)(2,1)S(1)} all-to-all(bf16[16,9,4,128]{3,2,1,0:T(4,128)(2,1)S(1)} %total.1), channel_id=1, replica_groups=mesh['tok'=64,'head'=16] {'head'}, dimensions={0} | all-to-all | bytes 294912 | tf_op jit(solution)/shard_map/all_to_all | solution.py:325
  68.0 0.7 %head_sum.1 = (bf16[8,512]{1,0:T(8,128)(2,1)}, bf16[8,64]{1,0:T(8,128)(2,1)}) custom-call(bf16[16,9,4,128]{3,2,1,0:T(4,128)(2,1)S(1)} %all_to_all.5.blocks_ref), custom_call_target="tpu_custom_call" | custom-call | bytes 200000 | tf_op jit(solution)/shard_map/head_sum/pallas_call | solution.py:302
Async XLA Ops:
  0.6 11.0 %copy-start = (bf16[128,512]{1,0:T(8,128)(2,1)S(1)}, bf16[128,512]{1,0:T(8,128)(2,1)}, u32[]{:S(2)}) copy-start(bf16[128,512]{1,0:T(8,128)(2,1)} %qr_ref.1) | copy-start | bytes 393220
  1.6 11.6 %collective-permute-start.2 = (bf16[144,512]{1,0:T(8,128)(2,1)S(1)}, bf16[144,512]{1,0:T(8,128)(2,1)S(1)}, u32[]{:S(2)}, u32[]{:S(2)}) collective-permute-start(bf16[144,512]{1,0:T(8,128)(2,1)S(1)} %pack.1.own_ref), channel_id=1, source_target_pairs={{0,32},{16,48},{32,64},{48,80},{64,96},{80,112},{96,128},{112,144}... | collective-permute-start | bytes 442376 | tf_op jit(solution)/shard_map/ppermute | solution.py:310
  5.1 11.1 %collective-permute-start.1 = (bf16[144,512]{1,0:T(8,128)(2,1)S(1)}, bf16[144,512]{1,0:T(8,128)(2,1)S(1)}, u32[]{:S(2)}, u32[]{:S(2)}) collective-permute-start(bf16[144,512]{1,0:T(8,128)(2,1)S(1)} %pack.1.own_ref), channel_id=1, source_target_pairs={{0,48},{16,64},{32,80},{48,96},{64,112},{80,128},{96,144},{112,160... | collective-permute-start | bytes 442376 | tf_op jit(solution)/shard_map/ppermute | solution.py:310
  7.8 10.4 %collective-permute-start = (bf16[144,512]{1,0:T(8,128)(2,1)S(1)}, bf16[144,512]{1,0:T(8,128)(2,1)S(1)}, u32[]{:S(2)}, u32[]{:S(2)}) collective-permute-start(bf16[144,512]{1,0:T(8,128)(2,1)S(1)} %pack.1.own_ref), channel_id=1, source_target_pairs={{0,16},{16,32},{32,48},{48,64},{64,80},{80,96},{96,112},{112,128},... | collective-permute-start | bytes 442376 | tf_op jit(solution)/shard_map/ppermute | solution.py:310
  21.4 10.9 %collective-permute-start.3 = (bf16[144,512]{1,0:T(8,128)(2,1)S(1)}, bf16[144,512]{1,0:T(8,128)(2,1)S(1)}, u32[]{:S(2)}, u32[]{:S(2)}) collective-permute-start(bf16[144,512]{1,0:T(8,128)(2,1)S(1)} %get-tuple-element.39), channel_id=1, source_target_pairs={{48,0},{64,16},{80,32},{96,48},{112,64},{128,80},{144,96},{160,112... | collective-permute-start | bytes 442376 | tf_op jit(solution)/shard_map/ppermute | solution.py:310
  23.4 9.6 %collective-permute-start.4 = (bf16[144,512]{1,0:T(8,128)(2,1)S(1)}, bf16[144,512]{1,0:T(8,128)(2,1)S(1)}, u32[]{:S(2)}, u32[]{:S(2)}) collective-permute-start(bf16[144,512]{1,0:T(8,128)(2,1)S(1)} %get-tuple-element.40), channel_id=1, source_target_pairs={{32,0},{48,16},{64,32},{80,48},{96,64},{112,80},{128,96},{144,112}... | collective-permute-start | bytes 442376 | tf_op jit(solution)/shard_map/ppermute | solution.py:310
  26.0 7.9 %collective-permute-start.5 = (bf16[144,512]{1,0:T(8,128)(2,1)S(1)}, bf16[144,512]{1,0:T(8,128)(2,1)S(1)}, u32[]{:S(2)}, u32[]{:S(2)}) collective-permute-start(bf16[144,512]{1,0:T(8,128)(2,1)S(1)} %get-tuple-element.41), channel_id=1, source_target_pairs={{16,0},{32,16},{48,32},{64,48},{80,64},{96,80},{112,96},{128,112},... | collective-permute-start | bytes 442376 | tf_op jit(solution)/shard_map/ppermute | solution.py:310

commit v7 on v6

--- a/solution.py
+++ b/solution.py
@@ -4,6 +4,7 @@
 from jax.experimental import pallas as pl
 from jax.experimental.pallas import tpu as pltpu
 from jax.sharding import PartitionSpec as P
+
 
 SPAN = 3
 
@@ -28,7 +29,6 @@
 F32 = jnp.float32
 BF16 = jnp.bfloat16
 VMEM = pltpu.MemorySpace.VMEM
-SMEM = pltpu.MemorySpace.SMEM
 HBM = pltpu.MemorySpace.HBM
 
 NT = (((1,), (1,)), ((), ()))
@@ -225,7 +225,7 @@
     return jax.ShapeDtypeStruct(dims, dtype)
 
 
-def call(kernel, outs, spaces, scratch=(), flops=0, moved=0, name=None, limit=24):
+def call(kernel, outs, spaces, scratch=(), flops=0, moved=0, limit=24):
     return pl.pallas_call(
         kernel,
         out_shape=outs,
@@ -234,7 +234,6 @@
         scratch_shapes=scratch,
         compiler_params=pltpu.CompilerParams(vmem_limit_bytes=limit << 20),
         cost_estimate=pl.CostEstimate(flops=flops, bytes_accessed=moved, transcendentals=0),
-        name=name,
     )
 
 
@@ -245,7 +244,7 @@
 def pack(latents, rotary_t):
     return call(
         pack_kernel, shape((PACK, DL)), [HBM] * 2,
-        scratch=[pltpu.SemaphoreType.DMA((1 + DL // TOK,))], moved=300000, name="pack",
+        scratch=[pltpu.SemaphoreType.DMA((1 + DL // TOK,))], moved=300000,
     )(latents, rotary_t)
 
 
@@ -258,7 +257,7 @@
             pltpu.VMEM((ROWS, 2 * DR), F32),
             pltpu.SemaphoreType.DMA((2 * FETCHES + 1,)),
         ],
-        moved=4 << 20, name="row_setup",
+        moved=4 << 20,
     )(lens, q, do, qr)
 
 
@@ -266,9 +265,7 @@
     outs = (
         shape((HALF, ROWS), F32), shape((HALF, ROWS), F32), shape((HALF, DL)), shape((HALF, 2 * DR)),
     )
-    return call(
-        near_kernel, outs, [VMEM] * 5, flops=2 * ROWS * KEYS * DL, moved=4 << 20, name="near_scores"
-    )(q, qx, do, own, k2)
+    return call(near_kernel, outs, [VMEM] * 5, flops=2 * ROWS * KEYS * DL, moved=4 << 20)(q, qx, do, own, k2)
 
 
 def scores(low, q, qx, do, k1, k3, raw, prob_grad, near, near2):
@@ -279,7 +276,7 @@
     )
     return call(
         scores_kernel, outs, [VMEM] * 10,
-        flops=2 * ROWS * KEYS * DL * 2, moved=6 << 20, name="scores",
+        flops=2 * ROWS * KEYS * DL * 2, moved=6 << 20,
     )(low, q, qx, do, k1, k3, raw, prob_grad, near, near2)
 
 
@@ -287,21 +284,17 @@
     outs = (shape((ROWS, DL)), shape((TOK, HEADS * DR)), shape((PACK, DL), F32))
     return call(
         queries_kernel, outs, [VMEM] * 7, scratch=[pltpu.VMEM((ROWS, 2 * DR), F32)],
-        flops=2 * ROWS * KEYS * DL * 2, moved=6 << 20, name="queries",
+        flops=2 * ROWS * KEYS * DL * 2, moved=6 << 20,
     )(q, qx, do, dst, pt, keys, rot2)
 
 
 def total(g0, r3, r2, r1, groups):
-    return call(
-        total_kernel, shape((groups, BLOCK, 4, TOK)), [VMEM] * 4, moved=1 << 20, name="total"
-    )(g0, r3, r2, r1)
+    return call(total_kernel, shape((groups, BLOCK, 4, TOK)), [VMEM] * 4, moved=1 << 20)(g0, r3, r2, r1)
 
 
 def head_sum(blocks):
     rows = TOK // blocks.shape[0]
-    return call(
-        sum_kernel, (shape((rows, DL)), shape((rows, DR))), [VMEM], moved=200000, name="head_sum"
-    )(blocks)
+    return call(sum_kernel, (shape((rows, DL)), shape((rows, DR))), [VMEM], moved=200000)(blocks)
 
 
 def shifted(block, axis, distance):
@@ -315,7 +308,10 @@
     q = query_latent.reshape(ROWS, DL)
     do = out_grad.reshape(ROWS, DL)
     own = pack(in_hbm(latents), in_hbm(key_rotary.T))
-    k1, k2, k3 = [shifted(own, "tok", distance) for distance in (1, 2, 3)]
+    fetched = []
+    for distance in (1, 2, 3):
+        fetched.append(shifted(own, "tok", distance))
+    k1, k2, k3 = fetched
     q, do, qx, low = row_setup(in_hbm(doc_lengths), in_hbm(q), in_hbm(do), query_rotary)
     raw, prob_grad, near, near2 = near_scores(q, qx, do, own, k2)
     f3, f2, f1, dst, pt, keys, rot2 = scores(low, q, qx, do, k1, k3, raw, prob_grad, near, near2)

time: 69.1 us -> 69.1 us (level)
  no operation moved by 1% of the time
where the time goes in v7:
time: 69.1 us; the launch traced here: 68.8 us
  blocking collectives  33.9 us (49%)
  starting transfers between devices  18.6 us (27%)
  Pallas kernels  9.99 us (14%)
  waiting for transfers between devices  5.51 us (8%)
  between operations  0.74 us (1%)
    all_to_all x1, blocking collectives, body(): lax.all_to_all(blocks, 'head', split_axis=0, concat_axis=0, tiled=True)  33.9 us
    ppermute x6, starting transfers between devices, shifted(): return lax.ppermute(block, axis, route)  18.6 us
    ppermute x6, waiting for transfers between devices, shifted(): return lax.ppermute(block, axis, route)  5.51 us
    pallas_call x1, Pallas kernels, scores(): call(scores_kernel, outs, [VMEM] * 10, flops=2 * ROWS * KEYS * DL * 2, mo...  3.24 us
    pallas_call x1, Pallas kernels, queries(): call(queries_kernel, outs, [VMEM] * 7, scratch=[pltpu.VMEM((ROWS, 2 * DR)...  2.33 us
    pallas_call x1, Pallas kernels, row_setup(): call(rows_kernel, outs, [HBM, HBM, HBM, VMEM], scratch=[pltpu.SMEM(lens.s...  1.6 us
  transfers between devices with their start and end apart: 6, of which 4 were waited for; matrix products, arithmetic and copies ran while one was open for 0% of the time, Pallas kernels for 7%

profile of v7, /device:TPU:68, one launch (start us, length us, event | category | flops | bytes accessed | tf_op | source)
XLA Modules:
  0.0 68.8 jit_solution(8252927064527592076)
XLA Ops:
  0.6 0.0 copy-start
  0.6 1.0 %shard_map.94.own_ref = bf16[144,512]{1,0:T(8,128)(2,1)S(1)} custom-call(bf16[128,512]{1,0:T(8,128)(2,1)} %lat_ref.1, bf16[64,128]{1,0:T(8,128)(2,1)} %bitcast.6), custom_call_target="tpu_custom_call" | custom-call | bytes 300000 | tf_op jit(solution)/shard_map/pallas_call | solution.py:245
  1.6 3.5 %collective-permute-start.2 = (bf16[144,512]{1,0:T(8,128)(2,1)S(1)}, bf16[144,512]{1,0:T(8,128)(2,1)S(1)}, u32[]{:S(2)}, u32[]{:S(2)}) collective-permute-start(bf16[144,512]{1,0:T(8,128)(2,1)S(1)} %shard_map.94.own_ref), channel_id=1, source_target_pairs={{0,32},{16,48},{32,64},{48,80},{64,96},{80,112},{96,128},{112,144}... | collective-permute-start | bytes 442376 | tf_op jit(solution)/shard_map/ppermute | solution.py:303
  5.1 2.6 %collective-permute-start.1 = (bf16[144,512]{1,0:T(8,128)(2,1)S(1)}, bf16[144,512]{1,0:T(8,128)(2,1)S(1)}, u32[]{:S(2)}, u32[]{:S(2)}) collective-permute-start(bf16[144,512]{1,0:T(8,128)(2,1)S(1)} %shard_map.94.own_ref), channel_id=1, source_target_pairs={{0,48},{16,64},{32,80},{48,96},{64,112},{80,128},{96,144},{112,160... | collective-permute-start | bytes 442376 | tf_op jit(solution)/shard_map/ppermute | solution.py:303
  7.8 3.9 %collective-permute-start = (bf16[144,512]{1,0:T(8,128)(2,1)S(1)}, bf16[144,512]{1,0:T(8,128)(2,1)S(1)}, u32[]{:S(2)}, u32[]{:S(2)}) collective-permute-start(bf16[144,512]{1,0:T(8,128)(2,1)S(1)} %shard_map.94.own_ref), channel_id=1, source_target_pairs={{0,16},{16,32},{32,48},{48,64},{64,80},{80,96},{96,112},{112,128},... | collective-permute-start | bytes 442376 | tf_op jit(solution)/shard_map/ppermute | solution.py:303
  11.7 0.0 copy-done
  11.7 1.6 %shard_map.93 = (bf16[1024,512]{1,0:T(8,128)(2,1)S(1)}, bf16[1024,512]{1,0:T(8,128)(2,1)S(1)}, bf16[1024,128]{1,0:T(8,128)(2,1)S(1)}, s32[1,1024]{1,0:T(1,128)S(1)}) custom-call(s32[33]{0:T(128)} %lens_ref.1, bf16[1024,512]{1,0:T(8,128)(2,1)} %bitcast.4, bf16[1024,512]{1,0:T(8,128)(2,1)} %bitcast.5, bf16[128,512]{1,0:T(8,128)(2,1)S(1)} %copy-done), custom_call_target="tpu_custom_call" | custom-call | bytes 4194304 | tf_op jit(solution)/shard_map/pallas_call | solution.py:253
  13.3 0.0 collective-permute-done.2.k2_ref
  13.3 0.9 %shard_map.95 = (f32[256,1024]{1,0:T(8,128)S(1)}, f32[256,1024]{1,0:T(8,128)S(1)}, bf16[256,512]{1,0:T(8,128)(2,1)S(1)}, bf16[256,128]{1,0:T(8,128)(2,1)S(1)}) custom-call(bf16[1024,512]{1,0:T(8,128)(2,1)S(1)} %get-tuple-element.24.q_ref, bf16[1024,128]{1,0:T(8,128)(2,1)S(1)} %get-tuple-element.25.qx_ref, bf16[1024,512]{1,0:T(8,128)(2,1)S(1)} %get-tuple-element.26.do_ref, ...), custom_call_target="tpu_custom_call" | custom-call | flops 536870912 | bytes 4194304 | tf_op jit(solution)/shard_map/pallas_call | solution.py:268
  14.2 2.1 %collective-permute-done.1.k3_ref = bf16[144,512]{1,0:T(8,128)(2,1)S(1)} collective-permute-done((bf16[144,512]{1,0:T(8,128)(2,1)S(1)}, bf16[144,512]{1,0:T(8,128)(2,1)S(1)}, u32[]{:S(2)}, u32[]{:S(2)}) %collective-permute-start.1) | collective-permute-done | bytes 147488 | tf_op jit(solution)/shard_map/ppermute | solution.py:303
  16.3 1.9 %collective-permute-done.k1_ref = bf16[144,512]{1,0:T(8,128)(2,1)S(1)} collective-permute-done((bf16[144,512]{1,0:T(8,128)(2,1)S(1)}, bf16[144,512]{1,0:T(8,128)(2,1)S(1)}, u32[]{:S(2)}, u32[]{:S(2)}) %collective-permute-start) | collective-permute-done | bytes 147488 | tf_op jit(solution)/shard_map/ppermute | solution.py:303
  18.2 3.2 %shard_map.96 = (bf16[144,512]{1,0:T(8,128)(2,1)S(1)}, bf16[144,512]{1,0:T(8,128)(2,1)S(1)}, bf16[144,512]{1,0:T(8,128)(2,1)S(1)}, bf16[512,1024]{1,0:T(8,128)(2...) custom-call(s32[1,1024]{1,0:T(1,128)S(1)} %get-tuple-element.27.low_ref, ...), custom_call_target="tpu_custom_call" | custom-call | flops 1073741824 | bytes 6291456 | tf_op jit(solution)/shard_map/pallas_call | solution.py:277
  21.4 1.9 %collective-permute-start.3 = (bf16[144,512]{1,0:T(8,128)(2,1)S(1)}, bf16[144,512]{1,0:T(8,128)(2,1)S(1)}, u32[]{:S(2)}, u32[]{:S(2)}) collective-permute-start(bf16[144,512]{1,0:T(8,128)(2,1)S(1)} %get-tuple-element.39), channel_id=1, source_target_pairs={{48,0},{64,16},{80,32},{96,48},{112,64},{128,80},{144,96},{160,112... | collective-permute-start | bytes 442376 | tf_op jit(solution)/shard_map/ppermute | solution.py:303
  23.4 2.7 %collective-permute-start.4 = (bf16[144,512]{1,0:T(8,128)(2,1)S(1)}, bf16[144,512]{1,0:T(8,128)(2,1)S(1)}, u32[]{:S(2)}, u32[]{:S(2)}) collective-permute-start(bf16[144,512]{1,0:T(8,128)(2,1)S(1)} %get-tuple-element.40), channel_id=1, source_target_pairs={{32,0},{48,16},{64,32},{80,48},{96,64},{112,80},{128,96},{144,112}... | collective-permute-start | bytes 442376 | tf_op jit(solution)/shard_map/ppermute | solution.py:303
  26.0 4.0 %collective-permute-start.5 = (bf16[144,512]{1,0:T(8,128)(2,1)S(1)}, bf16[144,512]{1,0:T(8,128)(2,1)S(1)}, u32[]{:S(2)}, u32[]{:S(2)}) collective-permute-start(bf16[144,512]{1,0:T(8,128)(2,1)S(1)} %get-tuple-element.41), channel_id=1, source_target_pairs={{16,0},{32,16},{48,32},{64,48},{80,64},{96,80},{112,96},{128,112},... | collective-permute-start | bytes 442376 | tf_op jit(solution)/shard_map/ppermute | solution.py:303
  30.0 2.3 %shard_map.97 = (bf16[1024,512]{1,0:T(8,128)(2,1)}, bf16[128,512]{1,0:T(8,128)(2,1)}, f32[144,512]{1,0:T(8,128)S(1)}) custom-call(bf16[1024,512]{1,0:T(8,128)(2,1)S(1)} %get-tuple-element.24.q_ref, bf16[1024,128]{1,0:T(8,128)(2,1)S(1)} %get-tuple-element.25.qx_ref, bf16[1024,512]{1,0:T(8,128)(2,1)S(1)} %get-tuple-element.26.do_ref, ...), custom_call_target="tpu_custom_call" | custom-call | flops 1073741824 | bytes 6291456 | tf_op jit(solution)/shard_map/pallas_call | solution.py:285
  32.4 0.0 collective-permute-done.3.r3_ref
  32.4 0.6 collective-permute-done.4.r2_ref
  33.0 0.9 %collective-permute-done.5.r1_ref = bf16[144,512]{1,0:T(8,128)(2,1)S(1)} collective-permute-done((bf16[144,512]{1,0:T(8,128)(2,1)S(1)}, bf16[144,512]{1,0:T(8,128)(2,1)S(1)}, u32[]{:S(2)}, u32[]{:S(2)}) %collective-permute-start.5) | collective-permute-done | bytes 147488 | tf_op jit(solution)/shard_map/ppermute | solution.py:303
  33.9 0.2 shard_map.98
  34.1 33.9 %all_to_all.5.blocks_ref = bf16[16,9,4,128]{3,2,1,0:T(4,128)(2,1)S(1)} all-to-all(bf16[16,9,4,128]{3,2,1,0:T(4,128)(2,1)S(1)} %shard_map.98), channel_id=1, replica_groups=mesh['tok'=64,'head'=16] {'head'}, dimensions={0} | all-to-all | bytes 294912 | tf_op jit(solution)/shard_map/all_to_all | solution.py:321
  68.0 0.7 %shard_map.99 = (bf16[8,512]{1,0:T(8,128)(2,1)}, bf16[8,64]{1,0:T(8,128)(2,1)}) custom-call(bf16[16,9,4,128]{3,2,1,0:T(4,128)(2,1)S(1)} %all_to_all.5.blocks_ref), custom_call_target="tpu_custom_call" | custom-call | bytes 200000 | tf_op jit(solution)/shard_map/pallas_call | solution.py:297
Async XLA Ops:
  0.6 11.0 %copy-start = (bf16[128,512]{1,0:T(8,128)(2,1)S(1)}, bf16[128,512]{1,0:T(8,128)(2,1)}, u32[]{:S(2)}) copy-start(bf16[128,512]{1,0:T(8,128)(2,1)} %qr_ref.1) | copy-start | bytes 393220
  1.6 11.6 %collective-permute-start.2 = (bf16[144,512]{1,0:T(8,128)(2,1)S(1)}, bf16[144,512]{1,0:T(8,128)(2,1)S(1)}, u32[]{:S(2)}, u32[]{:S(2)}) collective-permute-start(bf16[144,512]{1,0:T(8,128)(2,1)S(1)} %shard_map.94.own_ref), channel_id=1, source_target_pairs={{0,32},{16,48},{32,64},{48,80},{64,96},{80,112},{96,128},{112,144}... | collective-permute-start | bytes 442376 | tf_op jit(solution)/shard_map/ppermute | solution.py:303
  5.1 11.1 %collective-permute-start.1 = (bf16[144,512]{1,0:T(8,128)(2,1)S(1)}, bf16[144,512]{1,0:T(8,128)(2,1)S(1)}, u32[]{:S(2)}, u32[]{:S(2)}) collective-permute-start(bf16[144,512]{1,0:T(8,128)(2,1)S(1)} %shard_map.94.own_ref), channel_id=1, source_target_pairs={{0,48},{16,64},{32,80},{48,96},{64,112},{80,128},{96,144},{112,160... | collective-permute-start | bytes 442376 | tf_op jit(solution)/shard_map/ppermute | solution.py:303
  7.8 10.4 %collective-permute-start = (bf16[144,512]{1,0:T(8,128)(2,1)S(1)}, bf16[144,512]{1,0:T(8,128)(2,1)S(1)}, u32[]{:S(2)}, u32[]{:S(2)}) collective-permute-start(bf16[144,512]{1,0:T(8,128)(2,1)S(1)} %shard_map.94.own_ref), channel_id=1, source_target_pairs={{0,16},{16,32},{32,48},{48,64},{64,80},{80,96},{96,112},{112,128},... | collective-permute-start | bytes 442376 | tf_op jit(solution)/shard_map/ppermute | solution.py:303
  21.4 10.9 %collective-permute-start.3 = (bf16[144,512]{1,0:T(8,128)(2,1)S(1)}, bf16[144,512]{1,0:T(8,128)(2,1)S(1)}, u32[]{:S(2)}, u32[]{:S(2)}) collective-permute-start(bf16[144,512]{1,0:T(8,128)(2,1)S(1)} %get-tuple-element.39), channel_id=1, source_target_pairs={{48,0},{64,16},{80,32},{96,48},{112,64},{128,80},{144,96},{160,112... | collective-permute-start | bytes 442376 | tf_op jit(solution)/shard_map/ppermute | solution.py:303
  23.4 9.6 %collective-permute-start.4 = (bf16[144,512]{1,0:T(8,128)(2,1)S(1)}, bf16[144,512]{1,0:T(8,128)(2,1)S(1)}, u32[]{:S(2)}, u32[]{:S(2)}) collective-permute-start(bf16[144,512]{1,0:T(8,128)(2,1)S(1)} %get-tuple-element.40), channel_id=1, source_target_pairs={{32,0},{48,16},{64,32},{80,48},{96,64},{112,80},{128,96},{144,112}... | collective-permute-start | bytes 442376 | tf_op jit(solution)/shard_map/ppermute | solution.py:303
  26.0 7.9 %collective-permute-start.5 = (bf16[144,512]{1,0:T(8,128)(2,1)S(1)}, bf16[144,512]{1,0:T(8,128)(2,1)S(1)}, u32[]{:S(2)}, u32[]{:S(2)}) collective-permute-start(bf16[144,512]{1,0:T(8,128)(2,1)S(1)} %get-tuple-element.41), channel_id=1, source_target_pairs={{16,0},{32,16},{48,32},{64,48},{80,64},{96,80},{112,96},{128,112},... | collective-permute-start | bytes 442376 | tf_op jit(solution)/shard_map/ppermute | solution.py:303
